TPU v7x, 32 devices: a whole 2x2x4 slice. The times are simulated.
32 devices in a mesh: groups: 2 (over y), sess: 2 (over core), ctx: 8 (over z, x).
Axes of the slice: x: 2, y: 2, z: 4, core: 2. Of those that a mesh axis runs over, the one named last changes fastest.
Arguments:
- queries: bfloat16 [4, 8, 4096], P(('groups', 'sess'), 'ctx'), parts along dimension 0, may hold values from -12 to 12
- new_kv: bfloat16 [4, 8, 1024], P(('groups', 'sess'), 'ctx'), parts along dimension 0, may hold values from -8 to 8
- kv_pool: bfloat16 [64, 128, 1024], P(('groups', 'sess', 'ctx')), parts along dimension 0, may hold values from -6 to 6
- page_ids: int32 [4, 8, 2], P('groups', 'ctx'), parts along dimension 0, may hold values from 0 to 3, as said below
- cached_lengths: int32 [4], P('groups'), parts along dimension 0, may hold values from 512 to 2048, as said below
Outputs:
- attended: bfloat16 [4, 8, 4096], P(('groups', 'sess'), 'ctx'), parts along dimension 0
There are 2 independent parts, one for each index of `groups`. A program takes and returns all parts, laid end to end along the dimension named above; each array names one. Nothing has to cross between parts.
Inputs may be any that keep to these rules, and one draw needn't show every extreme that they name: For each context index c, the 4 entries page_ids[:, c, :] hold every number from 0 to 3 once; entry v names page v % 2 of the pool of session index v // 2 on the same context index. In some context index all pages of one session lie in the other session's pool. `cached_lengths`: some session has all 2048 positions cached.
All inputs are finite; a program needn't handle non-finite values.
Results may differ from a plain program's by a relative error of at most 0.0025.
Values may be sent and summed in bfloat16 or wider, within the bound.
No kernel may reach another device: no remote copies, remote signals or barrier semaphores. Data moves between devices by JAX's collectives and lax.ppermute only.
A program may use at most 64 MiB of HBM per device.

v0:
```python
import jax
import jax.numpy as jnp
from jax import lax
from jax.sharding import PartitionSpec as P

KVH = 4
HD = 128
GROUP = 8


masked_value = -1e30


def swapped(value, axis, distance):
    mask = 2**distance
    pairs = [(source, source ^ mask) for source in range(lax.axis_size(axis))]
    return lax.ppermute(value, axis, pairs)


def attend(carry_state, query_heads, key_rows, values, allowed):
    running, weight_sum, summed = carry_state
    scores = jnp.einsum(
        "qkgd,rkd->qkgr", query_heads, key_rows, preferred_element_type=jnp.float32
    ) * HD ** (-0.5)
    scores = jnp.where(allowed[:, None, None, :], scores, masked_value)
    highest = jnp.maximum(running, jnp.max(scores, axis=-1))
    factor = jnp.exp(running - highest)
    weights = jnp.exp(scores - highest[..., None])
    weight_sum = weight_sum * factor + jnp.sum(weights, axis=-1)
    summed = summed * factor[..., None] + jnp.einsum(
        "qkgr,rkd->qkgd", weights, values.astype(jnp.float32), preferred_element_type=jnp.float32
    )
    return (highest, weight_sum, summed)


def empty_state(query_heads):
    head_shape = query_heads.shape[:3]
    return (
        jnp.full(head_shape, masked_value, jnp.float32),
        jnp.zeros(head_shape, jnp.float32),
        jnp.zeros(query_heads.shape, jnp.float32),
    )


def cache_partial(query_heads, cache_rows, key_allowed):
    length = cache_rows.shape[0]
    block_rows = min(256, length)

    def advance(number, carry_state):
        kv_piece = cache_rows.reshape(block_rows, 2, KVH, HD)
        return attend(
            carry_state, query_heads, kv_piece[:, 0], kv_piece[:, 1], key_allowed[None, :]
        )

    return lax.fori_loop(0, length // block_rows, advance, empty_state(query_heads))


def settle(received):
    row_top, weight_sum, summed = received
    highest = jnp.max(row_top, axis=0)
    factor = jnp.exp(row_top - highest)
    weight_sum = jnp.sum(weight_sum * factor, axis=0)
    summed = jnp.sum(summed * factor[..., None], axis=0)
    return summed / weight_sum[..., None]


def body(queries, new_kv, kv_pool, page_ids, cached_lengths):
    session = lax.axis_index("sess")
    column = lax.axis_index("ctx")
    pool_pages = kv_pool.shape[0]
    page_len = kv_pool.shape[1]
    resident_rows = pool_pages * page_len
    gathered = lax.all_gather(queries, "ctx", axis=1, tiled=True)
    total_rows = gathered.shape[1]
    query_heads = gathered.reshape(total_rows, KVH, GROUP, HD)
    my_pages = jnp.take(page_ids[:, 0, :], session, axis=0)
    peer_pages = jnp.take(page_ids[:, 0, :], 1 - session, axis=0)
    my_length = jnp.take(cached_lengths, session)
    positions = column * resident_rows + jnp.arange(resident_rows, dtype=jnp.int32)
    my_owned = my_pages // pool_pages == session
    resident = jnp.take(kv_pool, my_pages % pool_pages, axis=0)
    peer_owned = peer_pages // pool_pages == session
    outgoing = jnp.where(
        peer_owned[:, None, None],
        jnp.take(kv_pool, peer_pages % pool_pages, axis=0),
        jnp.zeros((), kv_pool.dtype),
    )
    incoming = swapped(outgoing, "sess", 0)
    cache_rows = jnp.where(my_owned[:, None, None], resident, incoming).reshape(resident_rows, -1)
    carry_state = cache_partial(query_heads, cache_rows, positions < my_length)
    local_rows = new_kv.shape[1]
    new_rows = new_kv.reshape(local_rows, 2, KVH, HD)
    key_index = column * local_rows + jnp.arange(local_rows, dtype=jnp.int32)
    causal = key_index[None, :] <= jnp.arange(total_rows, dtype=jnp.int32)[:, None]
    carry_state = attend(carry_state, query_heads, new_rows[:, 0], new_rows[:, 1], causal)
    devices = lax.axis_size("ctx")
    row_top, weight_sum, summed = carry_state
    head_count = row_top.shape[1] * row_top.shape[2]
    result = settle(
        (
            lax.all_to_all(
                row_top.reshape(devices, local_rows, head_count),
                "ctx",
                split_axis=0,
                concat_axis=0,
                tiled=True,
            ),
            lax.all_to_all(
                weight_sum.reshape(devices, local_rows, head_count),
                "ctx",
                split_axis=0,
                concat_axis=0,
                tiled=True,
            ),
            lax.all_to_all(
                summed.reshape(devices, local_rows, head_count, -1),
                "ctx",
                split_axis=0,
                concat_axis=0,
                tiled=True,
            ),
        )
    )
    return result.reshape(1, local_rows, -1).astype(jnp.bfloat16)


def solution(mesh):
    placed = (
        P(("groups", "sess"), "ctx", None),
        P(("groups", "sess"), "ctx", None),
        P(("groups", "sess", "ctx"), None, None),
        P("groups", "ctx", None),
        P("groups"),
    )
    return jax.shard_map(
        body,
        mesh=mesh,
        in_specs=placed,
        out_specs=P(("groups", "sess"), "ctx", None),
        check_vma=False,
    )
```

profile of v0, /device:TPU:0, one launch (start us, length us, event | category | flops | bytes accessed | tf_op | source)
XLA Modules:
  0.0 72.6 jit_solution(1313129140245573123)
XLA Ops:
  0.0 0.0 copy-start
  0.0 0.0 copy-start.3
  0.0 0.7 %copy-done.3 = s32[2,1,2]{2,1,0:T(1,128)S(1)} copy-done((s32[2,1,2]{2,1,0:T(1,128)S(1)}, s32[2,1,2]{2,1,0:T(1,128)}, u32[]{:S(2)}) %copy-start.3) | copy-done | bytes 40
  0.8 0.3 copy-done
  1.1 0.6 gather_fusion.1
  1.6 0.1 select_select_fusion
  1.8 0.6 collective-permute-start
  2.4 0.0 copy-start.4
  2.4 0.0 copy-start.1
  2.4 0.6 gather_fusion
  3.0 0.0 copy-done.4
  3.0 0.7 dynamic-slice.6
  3.7 0.0 copy-done.1
  3.7 31.9 %all_gather.3 = bf16[1,8,4096]{2,0,1:T(2,128)(2,1)S(1)} all-gather(bf16[1,1,4096]{2,0,1:T(2,128)(2,1)S(1)} %bitcast.99), channel_id=1, replica_groups=mesh['groups'=2,'sess'=2,'ctx'=8] {'ctx'}, dimensions={1}, use_global_device_ids=true | all-gather | bytes 73728 | tf_op jit(solution)/shard_map/all_gather | solution.py:73
  35.6 0.0 copy-start.2
  35.6 0.4 reduce.3
  36.0 0.3 copy-done.2
  37.0 0.4 fusion.7
  37.4 0.0 collective-permute-done
  37.4 0.2 select_select_fusion.1
  37.5 0.4 reshape_reshape.4
  37.9 0.2 fusion.21
  38.1 0.3 fusion.22
  38.4 0.1 fusion.11
  38.5 0.2 fusion.5
  38.8 0.1 reduce_sum.41
  38.9 0.1 reduce_sum.42
  38.9 0.1 reduce_max.26
  39.0 0.1 max.55
  39.1 0.6 multiply_add_fusion
  39.7 11.7 %all_to_all.15 = f32[8,1,32]{2,1,0:T(1,128)S(1)} all-to-all(f32[8,1,32]{2,1,0:T(1,128)S(1)} %bitcast.101), channel_id=1, replica_groups=mesh['groups'=2,'sess'=2,'ctx'=8] {'ctx'}, dimensions={0} | all-to-all | bytes 2048 | tf_op jit(solution)/shard_map/all_to_all | solution.py:101
  51.4 3.3 %all-to-all-start.2 = ((f32[8,1,32]{2,1,0:T(1,128)}), f32[8,1,32]{2,1,0:T(1,128)S(1)}, u32[]{:S(2)}, u32[]{:S(2)}) async-start(f32[8,1,32]{2,1,0:T(1,128)} %bitcast.31), calls=%async_computation.2 | async-start | bytes 8192 | tf_op jit(solution)/shard_map/all_to_all | solution.py:108
  54.7 0.2 fusion.4
  55.0 0.6 copy.64
  55.6 5.5 %all-to-all-done.2 = f32[8,1,32]{2,1,0:T(1,128)S(1)} async-done(((f32[8,1,32]{2,1,0:T(1,128)}), f32[8,1,32]{2,1,0:T(1,128)S(1)}, u32[]{:S(2)}, u32[]{:S(2)}) %all-to-all-start.2) | async-done | bytes 1056 | tf_op jit(solution)/shard_map/all_to_all | solution.py:108
  61.1 3.4 %all-to-all-start = ((f32[8,1,32,128]{3,2,1,0:T(8,128)}), f32[8,1,32,128]{3,2,1,0:T(8,128)S(1)}, u32[]{:S(2)}, u32[]{:S(2)}) async-start(f32[8,1,32,128]{3,2,1,0:T(8,128)} %bitcast.93), calls=%async_computation | async-start | bytes 262144 | tf_op jit(solution)/shard_map/all_to_all | solution.py:115
  64.5 7.2 %all-to-all-done = f32[8,1,32,128]{3,2,1,0:T(8,128)S(1)} async-done(((f32[8,1,32,128]{3,2,1,0:T(8,128)}), f32[8,1,32,128]{3,2,1,0:T(8,128)S(1)}, u32[]{:S(2)}, u32[]{:S(2)}) %all-to-all-start) | async-done | bytes 131104 | tf_op jit(solution)/shard_map/all_to_all | solution.py:115
  71.8 0.1 multiply_reduce_fusion
  71.9 0.1 div.44
  71.9 0.6 divide_convert_fusion
  (17 shorter events, 0.2 us)
Async XLA Ops:
  0.0 1.1 %copy-start = (bf16[2,128,1024]{2,1,0:T(8,128)(2,1)S(1)}, bf16[2,128,1024]{2,1,0:T(8,128)(2,1)}, u32[]{:S(2)}) copy-start(bf16[2,128,1024]{2,1,0:T(8,128)(2,1)} %param.11) | copy-start | bytes 1572868
  0.0 0.7 %copy-start.3 = (s32[2,1,2]{2,1,0:T(1,128)S(1)}, s32[2,1,2]{2,1,0:T(1,128)}, u32[]{:S(2)}) copy-start(s32[2,1,2]{2,1,0:T(1,128)} %param.12) | copy-start | bytes 52
  1.8 35.6 %collective-permute-start = (bf16[2,128,1024]{2,1,0:T(8,128)(2,1)S(1)}, bf16[2,128,1024]{2,1,0:T(8,128)(2,1)S(1)}, u32[]{:S(2)}, u32[]{:S(2)}) collective-permute-start(bf16[2,128,1024]{2,1,0:T(8,128)(2,1)S(1)} %select_select_fusion), channel_id=1, source_target_pairs={{0,8},{8,0},{1,9},{9,1},{2,10},{10,2},{3,11},{11,3},{4,12},{12,4},... | collective-permute-start | bytes 1572872 | tf_op jit(solution)/shard_map/ppermute | solution.py:17
  2.4 0.7 copy-start.4
  2.4 1.3 %copy-start.1 = (bf16[1,1,4096]{2,1,0:T(2,128)(2,1)S(1)}, bf16[1,1,4096]{2,1,0:T(2,128)(2,1)}, u32[]{:S(2)}) copy-start(bf16[1,1,4096]{2,1,0:T(2,128)(2,1)} %param.9) | copy-start | bytes 24580
  35.6 0.7 copy-start.2
  51.4 9.7 %all-to-all-start.2 = ((f32[8,1,32]{2,1,0:T(1,128)}), f32[8,1,32]{2,1,0:T(1,128)S(1)}, u32[]{:S(2)}, u32[]{:S(2)}) async-start(f32[8,1,32]{2,1,0:T(1,128)} %bitcast.31), calls=%async_computation.2 | async-start | bytes 8192 | tf_op jit(solution)/shard_map/all_to_all | solution.py:108
  61.1 10.7 %all-to-all-start = ((f32[8,1,32,128]{3,2,1,0:T(8,128)}), f32[8,1,32,128]{3,2,1,0:T(8,128)S(1)}, u32[]{:S(2)}, u32[]{:S(2)}) async-start(f32[8,1,32,128]{3,2,1,0:T(8,128)} %bitcast.93), calls=%async_computation | async-start | bytes 262144 | tf_op jit(solution)/shard_map/all_to_all | solution.py:115
where the time goes:
time: 73 us; the launch traced here: 72.6 us
  blocking collectives  43.6 us (60%)
  waiting for transfers between devices  12.7 us (17%)
  starting transfers between devices  7.24 us (10%)
  local copies, waits for them, and re-layouts  4.81 us (7%)
  other arithmetic  2.45 us (3%)
  matrix products  0.91 us (1%)
  between operations  0.88 us (1%)
    all_gather x1, blocking collectives, body(): gathered = lax.all_gather(queries, 'ctx', axis=1, tiled=True)  31.9 us
    all_to_all x1, blocking collectives, body(): lax.all_to_all(row_top.reshape(devices, local_rows, head_count), 'ctx', s...  11.7 us
    all_to_all x1, waiting for transfers between devices, body(): lax.all_to_all(summed.reshape(devices, local_rows, head_count, -1), 'ctx'...  7.22 us
    all_to_all x1, waiting for transfers between devices, body(): lax.all_to_all(weight_sum.reshape(devices, local_rows, head_count), 'ctx'...  5.46 us
    all_to_all x1, starting transfers between devices, body(): lax.all_to_all(summed.reshape(devices, local_rows, head_count, -1), 'ctx'...  3.37 us
    all_to_all x1, starting transfers between devices, body(): lax.all_to_all(weight_sum.reshape(devices, local_rows, head_count), 'ctx'...  3.31 us
  transfers between devices with their start and end apart: 3, of which 2 were waited for; matrix products, arithmetic and copies ran while one was open for 4% of the time, Pallas kernels for 0%

commit v1 on v0

v1 whole, which is shorter than its diff:
```python
import functools

import jax
import jax.numpy as jnp
from jax import lax
from jax.experimental import pallas as pl
from jax.experimental.pallas import tpu as pltpu
from jax.sharding import PartitionSpec as P

KVH = 4
HD = 128
GROUP = 8
HQ = KVH * GROUP
STATE_ROWS = HQ + GROUP
masked_value = -1e30
GRANT = 2**24
VMEM = pltpu.VMEM
SMEM = pltpu.SMEM


def swapped(value, axis, mask):
    pairs = [(source, source ^ mask) for source in range(lax.axis_size(axis))]
    return lax.ppermute(value, axis, pairs)


def heads_kernel(own_ref, peer_ref, out_ref):
    for place, ref in enumerate((own_ref, peer_ref)):
        row = ref[0].astype(jnp.float32)
        out_ref[place * HQ : (place + 1) * HQ, :] = row.reshape(HQ, HD).astype(out_ref.dtype)


def join_kernel(own_ref, peer_ref, out_ref):
    rows = own_ref.shape[0]
    out_ref[:rows, :] = own_ref[...]
    out_ref[rows:, :] = peer_ref[...]


def pages_kernel(ids_ref, lengths_ref, pool_ref, peer_ref, cache_ref, bias_ref):
    session = lax.axis_index("sess")
    column = lax.axis_index("ctx")
    slots, page_len, _ = pool_ref.shape
    for slot in range(slots):
        ident = ids_ref[session, 0, slot]
        mine = (ident // slots) == session
        page = ident % slots
        cache_ref[slot * page_len : (slot + 1) * page_len, :] = jnp.where(
            mine, pool_ref[page], peer_ref[page]
        )
    rows = slots * page_len
    place = lax.broadcasted_iota(jnp.int32, bias_ref.shape, 1)
    left = lengths_ref[session] - column * rows
    bias_ref[...] = jnp.where(place < left, 0.0, masked_value)


def attend_kernel(own_ref, peer_ref, cache_ref, bias_ref, new_ref, out_ref):
    column = lax.axis_index("ctx")
    half = own_ref.shape[0] // HQ
    tokens = 2 * half
    own = own_ref[...].astype(jnp.float32)
    peer = peer_ref[...].astype(jnp.float32)
    bias = bias_ref[0:1, :]
    fresh = new_ref[0].astype(jnp.float32)
    place = lax.broadcasted_iota(jnp.int32, (GROUP, 1), 0)
    fresh_bias = jnp.concatenate(
        [jnp.where((place * 0 + (column ^ near)) >= column, 0.0, masked_value) for near in range(tokens)], axis=0
    )
    lane = lax.broadcasted_iota(jnp.int32, (tokens * GROUP, HD), 1)
    states = jnp.zeros((tokens * GROUP, HD), jnp.float32)
    for head in range(KVH):
        at = slice(head * HD, (head + 1) * HD)
        value_at = slice((KVH + head) * HD, (KVH + head + 1) * HD)
        query = jnp.concatenate(
            [
                part[near * HQ + head * GROUP : near * HQ + (head + 1) * GROUP]
                for part in (own, peer)
                for near in range(half)
            ],
            axis=0,
        )
        scores = lax.dot_general(
            query.astype(jnp.bfloat16), cache_ref[:, at], (((1,), (1,)), ((), ())),
            preferred_element_type=jnp.float32,
        )
        scores = scores * HD ** (-0.5) + bias
        fresh_scores = jnp.sum(query * fresh[:, at], axis=1, keepdims=True) * HD ** (-0.5) + fresh_bias
        top = jnp.maximum(jnp.max(scores, axis=1, keepdims=True), fresh_scores)
        weights = jnp.exp(scores - top)
        fresh_weights = jnp.exp(fresh_scores - top)
        total = jnp.sum(weights, axis=1, keepdims=True) + fresh_weights
        coarse = weights.astype(jnp.bfloat16)
        fine = (weights - coarse.astype(jnp.float32)).astype(jnp.bfloat16)
        values = cache_ref[:, value_at]
        summed = (
            jnp.dot(coarse, values, preferred_element_type=jnp.float32)
            + jnp.dot(fine, values, preferred_element_type=jnp.float32)
            + fresh_weights * fresh[:, value_at]
        )
        states = jnp.where(lane == head, top, states)
        states = jnp.where(lane == KVH + head, total, states)
        for near in range(tokens):
            out_ref[column ^ near, head * GROUP : (head + 1) * GROUP, :] = summed[near * GROUP : (near + 1) * GROUP]
    for near in range(tokens):
        out_ref[column ^ near, HQ:, :] = states[near * GROUP : (near + 1) * GROUP]


def settle_kernel(parts_ref, out_ref):
    devices = parts_ref.shape[0]
    tops = [parts_ref[source, HQ:, :] for source in range(devices)]
    highest = functools.reduce(jnp.maximum, tops)
    weight_sum = 0.0
    factors = []
    for states in tops:
        factor = jnp.exp(states - highest)
        factors.append(factor)
        weight_sum = weight_sum + pltpu.roll(states, HD - KVH, 1) * factor
    pieces = []
    for head in range(KVH):
        summed = 0.0
        for source in range(devices):
            summed = summed + parts_ref[source, head * GROUP : (head + 1) * GROUP, :] * factors[source][:, head : head + 1]
        pieces.append(summed / weight_sum[:, head : head + 1])
    result = jnp.concatenate(pieces, axis=0)
    out_ref[0] = result.reshape(1, HQ * HD).astype(out_ref.dtype)


def kernel_call(kernel, out_shape, in_spaces, *operands, name=None):
    shapes = out_shape if isinstance(out_shape, (tuple, list)) else (out_shape,)
    specs = [pl.BlockSpec(memory_space=VMEM) for _ in shapes]
    return pl.pallas_call(
        kernel,
        out_shape=out_shape,
        in_specs=[pl.BlockSpec(memory_space=space) for space in in_spaces],
        out_specs=specs if isinstance(out_shape, (tuple, list)) else specs[0],
        name=name,
        compiler_params=pltpu.CompilerParams(vmem_limit_bytes=GRANT),
    )(*operands)


def body(queries, new_kv, kv_pool, page_ids, cached_lengths):
    devices = lax.axis_size("ctx")
    shape = jax.ShapeDtypeStruct
    peer_queries = swapped(queries, "ctx", 1)
    peer_pool = swapped(kv_pool, "sess", 1)
    gathered = kernel_call(heads_kernel, shape((2 * HQ, HD), queries.dtype), [VMEM] * 2, queries, peer_queries, name="heads")
    slots, page_len, width = kv_pool.shape
    rows = slots * page_len
    cache, bias = kernel_call(
        pages_kernel,
        (shape((rows, width), kv_pool.dtype), shape((8, rows), jnp.float32)),
        [SMEM, SMEM, VMEM, VMEM], page_ids, cached_lengths, kv_pool, peer_pool, name="pages",
    )
    mask = 2
    received = swapped(gathered, "ctx", mask)
    while 2 * mask < devices:
        gathered = kernel_call(join_kernel, shape((2 * gathered.shape[0], HD), queries.dtype), [VMEM] * 2, gathered, received, name="join")
        mask *= 2
        received = swapped(gathered, "ctx", mask)
    states = kernel_call(
        attend_kernel, shape((devices, STATE_ROWS, HD), jnp.float32), [VMEM] * 5, gathered, received, cache, bias, new_kv, name="attend",
    )
    parts = lax.all_to_all(states, "ctx", split_axis=0, concat_axis=0, tiled=True)
    return kernel_call(settle_kernel, shape(queries.shape, queries.dtype), [VMEM], parts, name="settle")


def solution(mesh):
    placed = (
        P(("groups", "sess"), "ctx", None),
        P(("groups", "sess"), "ctx", None),
        P(("groups", "sess", "ctx"), None, None),
        P("groups", "ctx", None),
        P("groups"),
    )
    return jax.shard_map(body, mesh=mesh, in_specs=placed, out_specs=P(("groups", "sess"), "ctx", None), check_vma=False)
```

time: 73 us -> 30 us (0.41)
  blocking collectives: 43.6 us -> 13.7 us
  waiting for transfers between devices: 12.7 us -> 3.84 us
  local copies, waits for them, and re-layouts: 4.81 us -> 1.77 us
  other arithmetic: 2.45 us -> 0 us
  Pallas kernels: 0 us -> 2.24 us
  starting transfers between devices: 7.24 us -> 8.18 us
  matrix products: 0.91 us -> 0 us
  between operations: 0.88 us -> 0.04 us
    all_gather x1 -> x0, blocking collectives: 31.9 us -> none  [body(): gathered = lax.all_gather(queries, 'ctx', axis=1, tiled=True)]
    all_to_all x2 -> x0, waiting for transfers between devices: 12.7 us -> none  [the longest x1 7.22 us: body(): lax.all_to_all(summed.reshape(devices, local_rows, head_count, -1), 'ctx'...]
    ppermute x1 -> x4, starting transfers between devices: 0.56 us -> 8.18 us  [swapped(): return lax.ppermute(value, axis, pairs)]
    all_to_all x2 -> x0, starting transfers between devices: 6.68 us -> none  [the longest x1 3.37 us: body(): lax.all_to_all(summed.reshape(devices, local_rows, head_count, -1), 'ctx'...]
    ppermute x1 -> x4, waiting for transfers between devices: 0.01 us -> 3.84 us  [swapped(): return lax.ppermute(value, axis, pairs)]
    pallas_call x0 -> x5, Pallas kernels: none -> 2.24 us  [kernel_call(): pl.pallas_call(kernel, out_shape=out_shape, in_specs=[pl.BlockSpec(memory...]
    all_to_all x1, blocking collectives: 11.7 us -> 13.7 us  [body(): lax.all_to_all(states, 'ctx', split_axis=0, concat_axis=0, tiled=True)]
    gather x2 -> x0, local copies, waits for them, and re-layouts: 1.16 us -> none  [the longest x1 0.58 us: body(): resident = jnp.take(kv_pool, my_pages % pool_pages, axis=0)]
  transfers between devices with their start and end apart: 3 -> 4, of which waited for: 2 -> 3; matrix products, arithmetic and copies ran while one was open for 4% -> 0% of each run, Pallas kernels for 0% -> 2%
where the time goes in v1:
time: 30 us; the launch traced here: 29.8 us
  blocking collectives  13.7 us (46%)
  starting transfers between devices  8.18 us (27%)
  waiting for transfers between devices  3.84 us (13%)
  Pallas kernels  2.24 us (7%)
  local copies, waits for them, and re-layouts  1.77 us (6%)
    all_to_all x1, blocking collectives, body(): lax.all_to_all(states, 'ctx', split_axis=0, concat_axis=0, tiled=True)  13.7 us
    ppermute x4, starting transfers between devices, swapped(): return lax.ppermute(value, axis, pairs)  8.18 us
    ppermute x4, waiting for transfers between devices, swapped(): return lax.ppermute(value, axis, pairs)  3.84 us
    pallas_call x5, Pallas kernels, kernel_call(): pl.pallas_call(kernel, out_shape=out_shape, in_specs=[pl.BlockSpec(memory...  2.24 us
    unnamed x10, local copies, waits for them, and re-layouts  1.77 us
  transfers between devices with their start and end apart: 4, of which 3 were waited for; matrix products, arithmetic and copies ran while one was open for 0% of the time, Pallas kernels for 2%

profile of v1, /device:TPU:0, one launch (start us, length us, event | category | flops | bytes accessed | tf_op | source)
XLA Modules:
  0.0 29.8 jit_solution(6550940008150011184)
XLA Ops:
  0.0 0.5 %collective-permute-start.3 = (bf16[2,128,1024]{2,1,0:T(8,128)(2,1)}, bf16[2,128,1024]{2,1,0:T(8,128)(2,1)S(1)}, u32[]{:S(2)}, u32[]{:S(2)}) collective-permute-start(bf16[2,128,1024]{2,1,0:T(8,128)(2,1)} %pool_ref.1), channel_id=1, source_target_pairs={{0,8},{8,0},{1,9},{9,1},{2,10},{10,2},{3,11},{11,3},{4,12},{12,4},... | collective-permute-start | bytes 1572872 | tf_op jit(solution)/shard_map/ppermute | solution.py:23
  0.5 2.5 %collective-permute-start = (bf16[1,1,4096]{2,1,0:T(2,128)(2,1)}, bf16[1,1,4096]{2,1,0:T(2,128)(2,1)S(1)}, u32[]{:S(2)}, u32[]{:S(2)}) collective-permute-start(bf16[1,1,4096]{2,1,0:T(2,128)(2,1)} %own_ref.1), channel_id=1, source_target_pairs={{0,1},{1,0},{2,3},{3,2},{4,5},{5,4},{6,7},{7,6},{8,9},{9,8},{10,11... | collective-permute-start | bytes 24584 | tf_op jit(solution)/shard_map/ppermute | solution.py:23
  3.0 1.9 %collective-permute-done.peer_ref = bf16[1,1,4096]{2,1,0:T(2,128)(2,1)S(1)} collective-permute-done((bf16[1,1,4096]{2,1,0:T(2,128)(2,1)}, bf16[1,1,4096]{2,1,0:T(2,128)(2,1)S(1)}, u32[]{:S(2)}, u32[]{:S(2)}) %collective-permute-start) | collective-permute-done | bytes 8224 | tf_op jit(solution)/shard_map/ppermute | solution.py:23
  4.9 0.0 copy-start.1
  4.9 0.7 %copy-done.1 = bf16[1,1,4096]{2,1,0:T(2,128)(2,1)S(1)} copy-done((bf16[1,1,4096]{2,1,0:T(2,128)(2,1)S(1)}, bf16[1,1,4096]{2,1,0:T(2,128)(2,1)}, u32[]{:S(2)}) %copy-start.1) | copy-done | bytes 8216
  5.6 0.0 copy-start.3
  5.6 0.0 copy-start.4
  5.7 2.2 %collective-permute-start.1 = (bf16[64,128]{1,0:T(8,128)(2,1)S(1)}, bf16[64,128]{1,0:T(8,128)(2,1)S(1)}, u32[]{:S(2)}, u32[]{:S(2)}) collective-permute-start(bf16[64,128]{1,0:T(8,128)(2,1)S(1)} %heads.1.own_ref), channel_id=1, source_target_pairs={{0,2},{1,3},{2,0},{3,1},{4,6},{5,7},{6,4},{7,5},{8,10},{9,11},{10,... | collective-permute-start | bytes 49160 | tf_op jit(solution)/shard_map/ppermute | solution.py:23
  7.8 1.7 %collective-permute-done.1.peer_ref = bf16[64,128]{1,0:T(8,128)(2,1)S(1)} collective-permute-done((bf16[64,128]{1,0:T(8,128)(2,1)S(1)}, bf16[64,128]{1,0:T(8,128)(2,1)S(1)}, u32[]{:S(2)}, u32[]{:S(2)}) %collective-permute-start.1) | collective-permute-done | bytes 16416 | tf_op jit(solution)/shard_map/ppermute | solution.py:23
  9.5 3.0 %collective-permute-start.2 = (bf16[128,128]{1,0:T(8,128)(2,1)S(1)}, bf16[128,128]{1,0:T(8,128)(2,1)S(1)}, u32[]{:S(2)}, u32[]{:S(2)}) collective-permute-start(bf16[128,128]{1,0:T(8,128)(2,1)S(1)} %join.1.own_ref), channel_id=1, source_target_pairs={{0,4},{1,5},{2,6},{3,7},{4,0},{5,1},{6,2},{7,3},{8,12},{9,13},{10,... | collective-permute-start | bytes 98312 | tf_op jit(solution)/shard_map/ppermute | solution.py:23
  12.6 0.0 collective-permute-done.3.peer_ref
  12.6 0.0 copy-done.3
  12.6 0.0 copy-done.4
  12.6 0.0 copy-start
  12.6 1.0 %copy-done = bf16[2,128,1024]{2,1,0:T(8,128)(2,1)S(1)} copy-done((bf16[2,128,1024]{2,1,0:T(8,128)(2,1)S(1)}, bf16[2,128,1024]{2,1,0:T(8,128)(2,1)}, u32[]{:S(2)}) %copy-start) | copy-done | bytes 524312
  13.6 0.0 copy-start.2
  13.6 0.6 %pages.1 = (bf16[256,1024]{1,0:T(8,128)(2,1)S(1)}, f32[8,256]{1,0:T(8,128)S(1)}) custom-call(s32[2,1,2]{2,1,0:T(1,128)S(1)} %copy-done.3, s32[2]{0:T(128)S(1)} %copy-done.4, bf16[2,128,1024]{2,1,0:T(8,128)(2,1)S(1)} %copy-done, bf16[2,128,1024]{2,1,0:T(8,128)(2,1)S(1)} %collective-permute-done.3.peer_ref), custom_call_target="tpu_custom_call" | custom-call | tf_op jit(solution)/shard_map/pages/pallas_call | solution.py:129
  14.3 0.2 collective-permute-done.2.peer_ref
  14.5 0.0 copy-done.2
  14.5 0.8 %attend.1 = f32[8,40,128]{2,1,0:T(8,128)S(1)} custom-call(bf16[128,128]{1,0:T(8,128)(2,1)S(1)} %join.1.own_ref, bf16[128,128]{1,0:T(8,128)(2,1)S(1)} %collective-permute-done.2.peer_ref, bf16[256,1024]{1,0:T(8,128)(2,1)S(1)} %get-tuple-element.7.cache_ref, f32[8,256]{1,0:T(8,128)S(1)} %get-tuple-element.8.bias_ref, bf16[1,1,1024]{2,1,0:T(2,128)(2,1)S(1)} %copy-done.2), custom_call_target="tpu_custom_call" | custom-call | tf_op jit(solution)/shard_map/attend/pallas_call | solution.py:129
  15.3 13.7 %all_to_all.5.parts_ref = f32[8,40,128]{2,1,0:T(8,128)S(1)} all-to-all(f32[8,40,128]{2,1,0:T(8,128)S(1)} %attend.1), channel_id=1, replica_groups=mesh['groups'=2,'sess'=2,'ctx'=8] {'ctx'}, dimensions={0} | all-to-all | bytes 327680 | tf_op jit(solution)/shard_map/all_to_all | solution.py:161
  29.0 0.8 %settle.1 = bf16[1,1,4096]{2,1,0:T(2,128)(2,1)} custom-call(f32[8,40,128]{2,1,0:T(8,128)S(1)} %all_to_all.5.parts_ref), custom_call_target="tpu_custom_call" | custom-call | tf_op jit(solution)/shard_map/settle/pallas_call | solution.py:129
  (2 shorter events, 0.0 us)
Async XLA Ops:
  0.0 12.6 %collective-permute-start.3 = (bf16[2,128,1024]{2,1,0:T(8,128)(2,1)}, bf16[2,128,1024]{2,1,0:T(8,128)(2,1)S(1)}, u32[]{:S(2)}, u32[]{:S(2)}) collective-permute-start(bf16[2,128,1024]{2,1,0:T(8,128)(2,1)} %pool_ref.1), channel_id=1, source_target_pairs={{0,8},{8,0},{1,9},{9,1},{2,10},{10,2},{3,11},{11,3},{4,12},{12,4},... | collective-permute-start | bytes 1572872 | tf_op jit(solution)/shard_map/ppermute | solution.py:23
  0.5 4.4 %collective-permute-start = (bf16[1,1,4096]{2,1,0:T(2,128)(2,1)}, bf16[1,1,4096]{2,1,0:T(2,128)(2,1)S(1)}, u32[]{:S(2)}, u32[]{:S(2)}) collective-permute-start(bf16[1,1,4096]{2,1,0:T(2,128)(2,1)} %own_ref.1), channel_id=1, source_target_pairs={{0,1},{1,0},{2,3},{3,2},{4,5},{5,4},{6,7},{7,6},{8,9},{9,8},{10,11... | collective-permute-start | bytes 24584 | tf_op jit(solution)/shard_map/ppermute | solution.py:23
  4.9 0.7 %copy-start.1 = (bf16[1,1,4096]{2,1,0:T(2,128)(2,1)S(1)}, bf16[1,1,4096]{2,1,0:T(2,128)(2,1)}, u32[]{:S(2)}) copy-start(bf16[1,1,4096]{2,1,0:T(2,128)(2,1)} %own_ref.1) | copy-start | bytes 24580
  5.6 7.0 %copy-start.3 = (s32[2,1,2]{2,1,0:T(1,128)S(1)}, s32[2,1,2]{2,1,0:T(1,128)}, u32[]{:S(2)}) copy-start(s32[2,1,2]{2,1,0:T(1,128)} %ids_ref.1) | copy-start | bytes 52
  5.6 6.9 %copy-start.4 = (s32[2]{0:T(128)S(1)}, s32[2]{0:T(128)}, u32[]{:S(2)}) copy-start(s32[2]{0:T(128)} %lengths_ref.1) | copy-start | bytes 28
  5.7 3.9 %collective-permute-start.1 = (bf16[64,128]{1,0:T(8,128)(2,1)S(1)}, bf16[64,128]{1,0:T(8,128)(2,1)S(1)}, u32[]{:S(2)}, u32[]{:S(2)}) collective-permute-start(bf16[64,128]{1,0:T(8,128)(2,1)S(1)} %heads.1.own_ref), channel_id=1, source_target_pairs={{0,2},{1,3},{2,0},{3,1},{4,6},{5,7},{6,4},{7,5},{8,10},{9,11},{10,... | collective-permute-start | bytes 49160 | tf_op jit(solution)/shard_map/ppermute | solution.py:23
  9.5 4.9 %collective-permute-start.2 = (bf16[128,128]{1,0:T(8,128)(2,1)S(1)}, bf16[128,128]{1,0:T(8,128)(2,1)S(1)}, u32[]{:S(2)}, u32[]{:S(2)}) collective-permute-start(bf16[128,128]{1,0:T(8,128)(2,1)S(1)} %join.1.own_ref), channel_id=1, source_target_pairs={{0,4},{1,5},{2,6},{3,7},{4,0},{5,1},{6,2},{7,3},{8,12},{9,13},{10,... | collective-permute-start | bytes 98312 | tf_op jit(solution)/shard_map/ppermute | solution.py:23
  12.6 1.0 %copy-start = (bf16[2,128,1024]{2,1,0:T(8,128)(2,1)S(1)}, bf16[2,128,1024]{2,1,0:T(8,128)(2,1)}, u32[]{:S(2)}) copy-start(bf16[2,128,1024]{2,1,0:T(8,128)(2,1)} %pool_ref.1) | copy-start | bytes 1572868
  13.6 0.8 %copy-start.2 = (bf16[1,1,1024]{2,1,0:T(2,128)(2,1)S(1)}, bf16[1,1,1024]{2,1,0:T(2,128)(2,1)}, u32[]{:S(2)}) copy-start(bf16[1,1,1024]{2,1,0:T(2,128)(2,1)} %new_ref.1) | copy-start | bytes 6148

commit v2 on v1

--- a/solution.py
+++ b/solution.py
@@ -23,16 +23,10 @@
     return lax.ppermute(value, axis, pairs)
 
 
-def heads_kernel(own_ref, peer_ref, out_ref):
-    for place, ref in enumerate((own_ref, peer_ref)):
-        row = ref[0].astype(jnp.float32)
-        out_ref[place * HQ : (place + 1) * HQ, :] = row.reshape(HQ, HD).astype(out_ref.dtype)
-
-
-def join_kernel(own_ref, peer_ref, out_ref):
-    rows = own_ref.shape[0]
-    out_ref[:rows, :] = own_ref[...]
-    out_ref[rows:, :] = peer_ref[...]
+def spread_kernel(row_ref, out_ref):
+    row = row_ref[0].astype(jnp.float32).reshape(HQ, HD).astype(out_ref.dtype)
+    for place in range(out_ref.shape[0]):
+        out_ref[place] = row
 
 
 def pages_kernel(ids_ref, lengths_ref, pool_ref, peer_ref, cache_ref, bias_ref):
@@ -52,31 +46,20 @@
     bias_ref[...] = jnp.where(place < left, 0.0, masked_value)
 
 
-def attend_kernel(own_ref, peer_ref, cache_ref, bias_ref, new_ref, out_ref):
+def attend_kernel(turn, queries_ref, cache_ref, bias_ref, new_ref, out_ref):
     column = lax.axis_index("ctx")
-    half = own_ref.shape[0] // HQ
-    tokens = 2 * half
-    own = own_ref[...].astype(jnp.float32)
-    peer = peer_ref[...].astype(jnp.float32)
+    tokens = queries_ref.shape[0]
+    queries = queries_ref[...].astype(jnp.float32)
     bias = bias_ref[0:1, :]
     fresh = new_ref[0].astype(jnp.float32)
-    place = lax.broadcasted_iota(jnp.int32, (GROUP, 1), 0)
-    fresh_bias = jnp.concatenate(
-        [jnp.where((place * 0 + (column ^ near)) >= column, 0.0, masked_value) for near in range(tokens)], axis=0
-    )
+    row = lax.broadcasted_iota(jnp.int32, (tokens * GROUP, 1), 0)
+    fresh_bias = jnp.where((row // GROUP + turn) % tokens >= column, 0.0, masked_value)
     lane = lax.broadcasted_iota(jnp.int32, (tokens * GROUP, HD), 1)
     states = jnp.zeros((tokens * GROUP, HD), jnp.float32)
     for head in range(KVH):
         at = slice(head * HD, (head + 1) * HD)
         value_at = slice((KVH + head) * HD, (KVH + head + 1) * HD)
-        query = jnp.concatenate(
-            [
-                part[near * HQ + head * GROUP : near * HQ + (head + 1) * GROUP]
-                for part in (own, peer)
-                for near in range(half)
-            ],
-            axis=0,
-        )
+        query = queries[:, head * GROUP : (head + 1) * GROUP, :].reshape(tokens * GROUP, HD)
         scores = lax.dot_general(
             query.astype(jnp.bfloat16), cache_ref[:, at], (((1,), (1,)), ((), ())),
             preferred_element_type=jnp.float32,
@@ -97,10 +80,8 @@
         )
         states = jnp.where(lane == head, top, states)
         states = jnp.where(lane == KVH + head, total, states)
-        for near in range(tokens):
-            out_ref[column ^ near, head * GROUP : (head + 1) * GROUP, :] = summed[near * GROUP : (near + 1) * GROUP]
-    for near in range(tokens):
-        out_ref[column ^ near, HQ:, :] = states[near * GROUP : (near + 1) * GROUP]
+        out_ref[:, head * GROUP : (head + 1) * GROUP, :] = summed.reshape(tokens, GROUP, HD)
+    out_ref[:, HQ:, :] = states.reshape(tokens, GROUP, HD)
 
 
 def settle_kernel(parts_ref, out_ref):
@@ -136,12 +117,19 @@
     )(*operands)
 
 
+def exchanged(value, turn):
+    devices = lax.axis_size("ctx")
+    order = [(place + turn) % devices for place in range(devices)]
+    return lax.all_to_all(value, "ctx", split_axis=0, concat_axis=0, axis_index_groups=[order], tiled=True)
+
+
 def body(queries, new_kv, kv_pool, page_ids, cached_lengths):
     devices = lax.axis_size("ctx")
+    turn = devices // 2
     shape = jax.ShapeDtypeStruct
-    peer_queries = swapped(queries, "ctx", 1)
     peer_pool = swapped(kv_pool, "sess", 1)
-    gathered = kernel_call(heads_kernel, shape((2 * HQ, HD), queries.dtype), [VMEM] * 2, queries, peer_queries, name="heads")
+    spread = kernel_call(spread_kernel, shape((devices, HQ, HD), queries.dtype), [VMEM], queries, name="spread")
+    gathered = exchanged(spread, turn)
     slots, page_len, width = kv_pool.shape
     rows = slots * page_len
     cache, bias = kernel_call(
@@ -149,16 +137,10 @@
         (shape((rows, width), kv_pool.dtype), shape((8, rows), jnp.float32)),
         [SMEM, SMEM, VMEM, VMEM], page_ids, cached_lengths, kv_pool, peer_pool, name="pages",
     )
-    mask = 2
-    received = swapped(gathered, "ctx", mask)
-    while 2 * mask < devices:
-        gathered = kernel_call(join_kernel, shape((2 * gathered.shape[0], HD), queries.dtype), [VMEM] * 2, gathered, received, name="join")
-        mask *= 2
-        received = swapped(gathered, "ctx", mask)
     states = kernel_call(
-        attend_kernel, shape((devices, STATE_ROWS, HD), jnp.float32), [VMEM] * 5, gathered, received, cache, bias, new_kv, name="attend",
+        functools.partial(attend_kernel, turn), shape((devices, STATE_ROWS, HD), jnp.float32), [VMEM] * 4, gathered, cache, bias, new_kv, name="attend",
     )
-    parts = lax.all_to_all(states, "ctx", split_axis=0, concat_axis=0, tiled=True)
+    parts = exchanged(states, turn)
     return kernel_call(settle_kernel, shape(queries.shape, queries.dtype), [VMEM], parts, name="settle")
 
 

time: 30 us -> 24.7 us (0.82)
  blocking collectives: 13.7 us -> 9.2 us
  waiting for transfers between devices: 3.84 us -> 2.84 us
  Pallas kernels: 2.24 us -> 2.55 us
    ppermute x4 -> x1, starting transfers between devices: 8.18 us -> 0.49 us  [swapped(): return lax.ppermute(value, axis, pairs)]
    all_to_all x0 -> x1, starting transfers between devices: none -> 7.48 us  [exchanged(): lax.all_to_all(value, 'ctx', split_axis=0, concat_axis=0, axis_index_grou...]
    all_to_all x1, blocking collectives: 13.7 us -> 9.2 us  [exchanged(): lax.all_to_all(value, 'ctx', split_axis=0, concat_axis=0, axis_index_grou...]
    ppermute x4 -> x1, waiting for transfers between devices: 3.84 us -> 0.01 us  [swapped(): return lax.ppermute(value, axis, pairs)]
    all_to_all x0 -> x1, waiting for transfers between devices: none -> 2.84 us  [exchanged(): lax.all_to_all(value, 'ctx', split_axis=0, concat_axis=0, axis_index_grou...]
    pallas_call x5 -> x4, Pallas kernels: 2.24 us -> 2.55 us  [kernel_call(): pl.pallas_call(kernel, out_shape=out_shape, in_specs=[pl.BlockSpec(memory...]
  transfers between devices with their start and end apart: 4 -> 2, of which waited for: 3 -> 1; matrix products, arithmetic and copies ran while one was open for 0% -> 0% of each run, Pallas kernels for 2% -> 5%
where the time goes in v2:
time: 24.7 us; the launch traced here: 24.4 us
  blocking collectives  9.2 us (37%)
  starting transfers between devices  7.98 us (32%)
  waiting for transfers between devices  2.84 us (11%)
  Pallas kernels  2.55 us (10%)
  local copies, waits for them, and re-layouts  1.76 us (7%)
    all_to_all x1, blocking collectives, exchanged(): lax.all_to_all(value, 'ctx', split_axis=0, concat_axis=0, axis_index_grou...  9.2 us
    all_to_all x1, starting transfers between devices, exchanged(): lax.all_to_all(value, 'ctx', split_axis=0, concat_axis=0, axis_index_grou...  7.48 us
    all_to_all x1, waiting for transfers between devices, exchanged(): lax.all_to_all(value, 'ctx', split_axis=0, concat_axis=0, axis_index_grou...  2.84 us
    pallas_call x4, Pallas kernels, kernel_call(): pl.pallas_call(kernel, out_shape=out_shape, in_specs=[pl.BlockSpec(memory...  2.55 us
    unnamed x10, local copies, waits for them, and re-layouts  1.76 us
  transfers between devices with their start and end apart: 2, of which 1 were waited for; matrix products, arithmetic and copies ran while one was open for 0% of the time, Pallas kernels for 5%

profile of v2, /device:TPU:0, one launch (start us, length us, event | category | flops | bytes accessed | tf_op | source)
XLA Modules:
  0.0 24.4 jit_solution(12445171410926788506)
XLA Ops:
  0.0 0.5 %collective-permute-start = (bf16[2,128,1024]{2,1,0:T(8,128)(2,1)}, bf16[2,128,1024]{2,1,0:T(8,128)(2,1)S(1)}, u32[]{:S(2)}, u32[]{:S(2)}) collective-permute-start(bf16[2,128,1024]{2,1,0:T(8,128)(2,1)} %pool_ref.1), channel_id=1, source_target_pairs={{0,8},{8,0},{1,9},{9,1},{2,10},{10,2},{3,11},{11,3},{4,12},{12,4},... | collective-permute-start | bytes 1572872 | tf_op jit(solution)/shard_map/ppermute | solution.py:23
  0.5 0.0 copy-start.1
  0.5 0.7 %copy-done.1 = bf16[1,1,4096]{2,1,0:T(2,128)(2,1)S(1)} copy-done((bf16[1,1,4096]{2,1,0:T(2,128)(2,1)S(1)}, bf16[1,1,4096]{2,1,0:T(2,128)(2,1)}, u32[]{:S(2)}) %copy-start.1) | copy-done | bytes 8216
  1.2 0.6 %spread.1 = bf16[8,32,128]{2,1,0:T(8,128)(2,1)} custom-call(bf16[1,1,4096]{2,1,0:T(2,128)(2,1)S(1)} %copy-done.1), custom_call_target="tpu_custom_call" | custom-call | tf_op jit(solution)/shard_map/spread/pallas_call | solution.py:110
  1.9 0.0 copy-start.3
  1.9 0.0 copy-start.4
  1.9 7.5 %all-to-all-start = ((bf16[8,32,128]{2,1,0:T(8,128)(2,1)}), bf16[8,32,128]{2,1,0:T(8,128)(2,1)S(1)}, u32[]{:S(2)}, u32[]{:S(2)}) async-start(bf16[8,32,128]{2,1,0:T(8,128)(2,1)} %spread.1), calls=%async_computation | async-start | bytes 131072 | tf_op jit(solution)/shard_map/all_to_all | solution.py:123
  9.3 0.0 collective-permute-done.peer_ref
  9.3 0.0 copy-done.3
  9.4 0.0 copy-done.4
  9.4 0.0 copy-start
  9.4 1.0 %copy-done = bf16[2,128,1024]{2,1,0:T(8,128)(2,1)S(1)} copy-done((bf16[2,128,1024]{2,1,0:T(8,128)(2,1)S(1)}, bf16[2,128,1024]{2,1,0:T(8,128)(2,1)}, u32[]{:S(2)}) %copy-start) | copy-done | bytes 524312
  10.4 0.0 copy-start.2
  10.4 0.6 %pages.1 = (bf16[256,1024]{1,0:T(8,128)(2,1)S(1)}, f32[8,256]{1,0:T(8,128)S(1)}) custom-call(s32[2,1,2]{2,1,0:T(1,128)S(1)} %copy-done.3, s32[2]{0:T(128)S(1)} %copy-done.4, bf16[2,128,1024]{2,1,0:T(8,128)(2,1)S(1)} %copy-done, bf16[2,128,1024]{2,1,0:T(8,128)(2,1)S(1)} %collective-permute-done.peer_ref), custom_call_target="tpu_custom_call" | custom-call | tf_op jit(solution)/shard_map/pages/pallas_call | solution.py:110
  11.0 2.8 %all-to-all-done.queries_ref = bf16[8,32,128]{2,1,0:T(8,128)(2,1)S(1)} async-done(((bf16[8,32,128]{2,1,0:T(8,128)(2,1)}), bf16[8,32,128]{2,1,0:T(8,128)(2,1)S(1)}, u32[]{:S(2)}, u32[]{:S(2)}) %all-to-all-start) | async-done | bytes 65568 | tf_op jit(solution)/shard_map/all_to_all | solution.py:123
  13.9 0.0 copy-done.2
  13.9 0.5 %attend.1 = f32[8,40,128]{2,1,0:T(8,128)S(1)} custom-call(bf16[8,32,128]{2,1,0:T(8,128)(2,1)S(1)} %all-to-all-done.queries_ref, bf16[256,1024]{1,0:T(8,128)(2,1)S(1)} %get-tuple-element.7.cache_ref, f32[8,256]{1,0:T(8,128)S(1)} %get-tuple-element.8.bias_ref, bf16[1,1,1024]{2,1,0:T(2,128)(2,1)S(1)} %copy-done.2), custom_call_target="tpu_custom_call" | custom-call | tf_op jit(solution)/shard_map/attend/pallas_call | solution.py:110
  14.4 9.2 %all_to_all.10.parts_ref = f32[8,40,128]{2,1,0:T(8,128)S(1)} all-to-all(f32[8,40,128]{2,1,0:T(8,128)S(1)} %attend.1), channel_id=1, replica_groups={{4,5,6,7,0,1,2,3},{12,13,14,15,8,9,10,11},{20,21,22,23,16,17,18,19},{28..., dimensions={0} | all-to-all | bytes 327680 | tf_op jit(solution)/shard_map/all_to_all | solution.py:123
  23.6 0.8 %settle.1 = bf16[1,1,4096]{2,1,0:T(2,128)(2,1)} custom-call(f32[8,40,128]{2,1,0:T(8,128)S(1)} %all_to_all.10.parts_ref), custom_call_target="tpu_custom_call" | custom-call | tf_op jit(solution)/shard_map/settle/pallas_call | solution.py:110
Async XLA Ops:
  0.0 9.3 %collective-permute-start = (bf16[2,128,1024]{2,1,0:T(8,128)(2,1)}, bf16[2,128,1024]{2,1,0:T(8,128)(2,1)S(1)}, u32[]{:S(2)}, u32[]{:S(2)}) collective-permute-start(bf16[2,128,1024]{2,1,0:T(8,128)(2,1)} %pool_ref.1), channel_id=1, source_target_pairs={{0,8},{8,0},{1,9},{9,1},{2,10},{10,2},{3,11},{11,3},{4,12},{12,4},... | collective-permute-start | bytes 1572872 | tf_op jit(solution)/shard_map/ppermute | solution.py:23
  0.5 0.7 %copy-start.1 = (bf16[1,1,4096]{2,1,0:T(2,128)(2,1)S(1)}, bf16[1,1,4096]{2,1,0:T(2,128)(2,1)}, u32[]{:S(2)}) copy-start(bf16[1,1,4096]{2,1,0:T(2,128)(2,1)} %row_ref.1) | copy-start | bytes 24580
  1.9 7.5 %copy-start.3 = (s32[2,1,2]{2,1,0:T(1,128)S(1)}, s32[2,1,2]{2,1,0:T(1,128)}, u32[]{:S(2)}) copy-start(s32[2,1,2]{2,1,0:T(1,128)} %ids_ref.1) | copy-start | bytes 52
  1.9 7.5 %copy-start.4 = (s32[2]{0:T(128)S(1)}, s32[2]{0:T(128)}, u32[]{:S(2)}) copy-start(s32[2]{0:T(128)} %lengths_ref.1) | copy-start | bytes 28
  1.9 12.0 %all-to-all-start = ((bf16[8,32,128]{2,1,0:T(8,128)(2,1)}), bf16[8,32,128]{2,1,0:T(8,128)(2,1)S(1)}, u32[]{:S(2)}, u32[]{:S(2)}) async-start(bf16[8,32,128]{2,1,0:T(8,128)(2,1)} %spread.1), calls=%async_computation | async-start | bytes 131072 | tf_op jit(solution)/shard_map/all_to_all | solution.py:123
  9.4 1.0 %copy-start = (bf16[2,128,1024]{2,1,0:T(8,128)(2,1)S(1)}, bf16[2,128,1024]{2,1,0:T(8,128)(2,1)}, u32[]{:S(2)}) copy-start(bf16[2,128,1024]{2,1,0:T(8,128)(2,1)} %pool_ref.1) | copy-start | bytes 1572868
  10.4 3.5 %copy-start.2 = (bf16[1,1,1024]{2,1,0:T(2,128)(2,1)S(1)}, bf16[1,1,1024]{2,1,0:T(2,128)(2,1)}, u32[]{:S(2)}) copy-start(bf16[1,1,1024]{2,1,0:T(2,128)(2,1)} %new_ref.1) | copy-start | bytes 6148

commit v3 on v2

v3 whole, which is shorter than its diff:
```python
import functools

import jax
import jax.numpy as jnp
from jax import lax
from jax.experimental import pallas as pl
from jax.experimental.pallas import tpu as pltpu
from jax.sharding import PartitionSpec as P

KVH = 4
HD = 128
GROUP = 8
HQ = KVH * GROUP
STATE_ROWS = HQ + GROUP
masked_value = -1e30
GRANT = 2**24
VMEM = pltpu.VMEM
SMEM = pltpu.SMEM


def swapped(value, axis, mask):
    pairs = [(source, source ^ mask) for source in range(lax.axis_size(axis))]
    return lax.ppermute(value, axis, pairs)


def prepare_kernel(
    row_hbm, new_hbm, pool_hbm, ids_hbm, lengths_hbm, out_ref, new_ref, pool_ref, bias_ref, pick_ref, row_ref, fresh_ref, ids_ref, lengths_ref, sems
):
    slots, page_len, _ = pool_ref.shape
    moves = [(row_hbm, row_ref), (ids_hbm, ids_ref), (lengths_hbm, lengths_ref), (new_hbm, fresh_ref), (pool_hbm, pool_ref)]
    copies = [pltpu.make_async_copy(source, target, sems.at[place]) for place, (source, target) in enumerate(moves)]
    for copy in copies:
        copy.start()
    session = lax.axis_index("sess")
    column = lax.axis_index("ctx")
    copies[0].wait()
    row = row_ref[0].astype(jnp.float32).reshape(HQ, HD).astype(out_ref.dtype)
    for place in range(out_ref.shape[0]):
        out_ref[place] = row
    copies[1].wait()
    copies[2].wait()
    left = lengths_ref[session] - column * slots * page_len
    lane = lax.broadcasted_iota(jnp.int32, bias_ref.shape, 1)
    bias_ref[...] = jnp.where(lane < left, 0.0, masked_value)
    for slot in range(slots):
        ident = ids_ref[session, 0, slot]
        physical = (ident // slots ^ session) * slots + ident % slots
        for page in range(1, 2 * slots):
            pick_ref[slot, page] = jnp.full(pick_ref.shape[2:], jnp.where(physical == page, 1.0, 0.0), jnp.float32).astype(pick_ref.dtype)
    copies[3].wait()
    new_ref[...] = fresh_ref[0].astype(jnp.float32).reshape(2 * KVH, HD)
    copies[4].wait()


def attend_kernel(first, second, queries_ref, pool_ref, peer_ref, bias_ref, pick_ref, new_ref, out_ref):
    column = lax.axis_index("ctx")
    tokens = queries_ref.shape[0]
    queries = queries_ref[...].astype(jnp.float32)
    bias = bias_ref[0:1, :]
    slots, page_len, _ = pool_ref.shape
    picked = [[None] + [jnp.concatenate([pick_ref[slot, page]] * (page_len // 16)) != 0 for page in range(1, 2 * slots)] for slot in range(slots)]
    row = lax.broadcasted_iota(jnp.int32, (tokens * GROUP, 1), 0)
    token = row // GROUP
    for place, value in enumerate(first):
        token = jnp.where(row // GROUP == place, value, token)
    fresh_bias = jnp.where(token >= column, 0.0, masked_value)
    pages = [(ref, page) for ref in (pool_ref, peer_ref) for page in range(ref.shape[0])]

    def chosen(slot, where):
        value = pages[0][0][pages[0][1], :, where]
        for mask, (ref, page) in zip(picked[slot][1:], pages[1:]):
            value = jnp.where(mask, ref[page, :, where], value)
        return value

    lane = lax.broadcasted_iota(jnp.int32, (tokens * GROUP, HD), 1)
    states = jnp.zeros((tokens * GROUP, HD), jnp.float32)
    for head in range(KVH):
        at = slice(head * HD, (head + 1) * HD)
        value_at = slice((KVH + head) * HD, (KVH + head + 1) * HD)
        query = queries[:, head * GROUP : (head + 1) * GROUP, :].reshape(tokens * GROUP, HD)
        keys, values = (jnp.concatenate([chosen(slot, where) for slot in range(slots)], axis=0) for where in (at, value_at))
        scores = lax.dot_general(
            query.astype(jnp.bfloat16), keys, (((1,), (1,)), ((), ())), preferred_element_type=jnp.float32
        )
        scores = scores * HD ** (-0.5) + bias
        fresh_scores = jnp.sum(query * new_ref[head : head + 1, :], axis=1, keepdims=True) * HD ** (-0.5) + fresh_bias
        top = jnp.maximum(jnp.max(scores, axis=1, keepdims=True), fresh_scores)
        weights = jnp.exp(scores - top)
        fresh_weights = jnp.exp(fresh_scores - top)
        total = jnp.sum(weights, axis=1, keepdims=True) + fresh_weights
        coarse = weights.astype(jnp.bfloat16)
        fine = (weights - coarse.astype(jnp.float32)).astype(jnp.bfloat16)
        summed = (
            jnp.dot(coarse, values, preferred_element_type=jnp.float32)
            + jnp.dot(fine, values, preferred_element_type=jnp.float32)
            + fresh_weights * new_ref[KVH + head : KVH + head + 1, :]
        )
        states = jnp.where(lane == head, top, states)
        states = jnp.where(lane == KVH + head, total, states)
        for place, value in enumerate(first):
            out_ref[second.index(value), head * GROUP : (head + 1) * GROUP, :] = summed[place * GROUP : (place + 1) * GROUP]
    for place, value in enumerate(first):
        out_ref[second.index(value), HQ:, :] = states[place * GROUP : (place + 1) * GROUP]


def settle_kernel(parts_ref, out_ref):
    devices = parts_ref.shape[0]
    tops = [parts_ref[source, HQ:, :] for source in range(devices)]
    highest = functools.reduce(jnp.maximum, tops)
    weight_sum = 0.0
    factors = []
    for states in tops:
        factor = jnp.exp(states - highest)
        factors.append(factor)
        weight_sum = weight_sum + pltpu.roll(states, HD - KVH, 1) * factor
    pieces = []
    for head in range(KVH):
        summed = 0.0
        for source in range(devices):
            summed = summed + parts_ref[source, head * GROUP : (head + 1) * GROUP, :] * factors[source][:, head : head + 1]
        pieces.append(summed / weight_sum[:, head : head + 1])
    result = jnp.concatenate(pieces, axis=0)
    out_ref[0] = result.reshape(1, HQ * HD).astype(out_ref.dtype)


def kernel_call(kernel, out_shape, *operands, name, space=VMEM, scratch=()):
    return pl.pallas_call(
        kernel,
        out_shape=out_shape,
        in_specs=[pl.BlockSpec(memory_space=space) for _ in operands],
        out_specs=jax.tree.map(lambda _: pl.BlockSpec(memory_space=VMEM), out_shape),
        scratch_shapes=scratch,
        name=name,
        compiler_params=pltpu.CompilerParams(vmem_limit_bytes=GRANT),
    )(*operands)


def exchanged(value, order):
    return lax.all_to_all(value, "ctx", split_axis=0, concat_axis=0, axis_index_groups=[order], tiled=True)


def body(queries, new_kv, kv_pool, page_ids, cached_lengths):
    devices = lax.axis_size("ctx")
    first = second = [(devices // 2 + 1 - place) % devices for place in range(devices)]
    shape = jax.ShapeDtypeStruct
    peer_pool = swapped(kv_pool, "sess", 1)
    slots, page_len, width = kv_pool.shape
    spread, fresh, pool, bias, pick = kernel_call(
        prepare_kernel,
        (
            shape((devices, HQ, HD), queries.dtype),
            shape((2 * KVH, HD), jnp.float32),
            shape(kv_pool.shape, kv_pool.dtype),
            shape((8, slots * page_len), jnp.float32),
            shape((slots, 2 * slots, 16, HD), kv_pool.dtype),
        ),
        *(pltpu.with_memory_space_constraint(value, pltpu.HBM) for value in (queries, new_kv, kv_pool, page_ids, cached_lengths)), name="prepare", space=pltpu.HBM,
        scratch=[
            VMEM(queries.shape, queries.dtype), VMEM(new_kv.shape, new_kv.dtype), SMEM(page_ids.shape, jnp.int32),
            SMEM(cached_lengths.shape, jnp.int32), pltpu.SemaphoreType.DMA((5,)),
        ],
    )
    gathered = exchanged(spread, first)
    states = kernel_call(
        functools.partial(attend_kernel, first, second), shape((devices, STATE_ROWS, HD), jnp.float32),
        gathered, pool, peer_pool, bias, pick, fresh, name="attend",
    )
    parts = exchanged(states, second)
    return kernel_call(settle_kernel, shape(queries.shape, queries.dtype), parts, name="settle")


def solution(mesh):
    placed = (
        P(("groups", "sess"), "ctx", None),
        P(("groups", "sess"), "ctx", None),
        P(("groups", "sess", "ctx"), None, None),
        P("groups", "ctx", None),
        P("groups"),
    )
    return jax.shard_map(body, mesh=mesh, in_specs=placed, out_specs=P(("groups", "sess"), "ctx", None), check_vma=False)
```

time: 24.7 us -> 22.6 us (0.915)
  blocking collectives: 9.2 us -> 19.4 us
  starting transfers between devices: 7.98 us -> 0.49 us
  waiting for transfers between devices: 2.84 us -> 0.01 us
  local copies, waits for them, and re-layouts: 1.76 us -> 0 us
    all_to_all x1 -> x2, blocking collectives: 9.2 us -> 19.4 us  [exchanged(): lax.all_to_all(value, 'ctx', split_axis=0, concat_axis=0, axis_index_grou...]
    all_to_all x1 -> x0, starting transfers between devices: 7.48 us -> none  [exchanged(): lax.all_to_all(value, 'ctx', split_axis=0, concat_axis=0, axis_index_grou...]
    all_to_all x1 -> x0, waiting for transfers between devices: 2.84 us -> none  [exchanged(): lax.all_to_all(value, 'ctx', split_axis=0, concat_axis=0, axis_index_grou...]
    unnamed x10 -> x0, local copies, waits for them, and re-layouts: 1.76 us -> none
    pallas_call x4 -> x3, Pallas kernels: 2.55 us -> 2.43 us  [kernel_call(): pl.pallas_call(kernel, out_shape=out_shape, in_specs=[pl.BlockSpec(memory...]
  transfers between devices with their start and end apart: 2 -> 1, of which waited for: 1 -> 0; matrix products, arithmetic and copies ran while one was open for 0% -> 0% of each run, Pallas kernels for 5% -> 5%
where the time goes in v3:
time: 22.6 us; the launch traced here: 22.3 us
  blocking collectives  19.4 us (86%)
  Pallas kernels  2.43 us (11%)
  starting transfers between devices  0.49 us (2%)
    all_to_all x2, blocking collectives, exchanged(): lax.all_to_all(value, 'ctx', split_axis=0, concat_axis=0, axis_index_grou...  19.4 us
    pallas_call x3, Pallas kernels, kernel_call(): pl.pallas_call(kernel, out_shape=out_shape, in_specs=[pl.BlockSpec(memory...  2.43 us
    ppermute x1, starting transfers between devices, swapped(): return lax.ppermute(value, axis, pairs)  0.49 us
  transfers between devices with their start and end apart: 1, of which 0 were waited for; matrix products, arithmetic and copies ran while one was open for 0% of the time, Pallas kernels for 5%

profile of v3, /device:TPU:0, one launch (start us, length us, event | category | flops | bytes accessed | tf_op | source)
XLA Modules:
  0.0 22.3 jit_solution(2057933047509154098)
XLA Ops:
  0.0 0.5 %collective-permute-start = (bf16[2,128,1024]{2,1,0:T(8,128)(2,1)}, bf16[2,128,1024]{2,1,0:T(8,128)(2,1)S(1)}, u32[]{:S(2)}, u32[]{:S(2)}) collective-permute-start(bf16[2,128,1024]{2,1,0:T(8,128)(2,1)} %pool_hbm.1), channel_id=1, source_target_pairs={{0,8},{8,0},{1,9},{9,1},{2,10},{10,2},{3,11},{11,3},{4,12},{12,4},... | collective-permute-start | bytes 1572872 | tf_op jit(solution)/shard_map/ppermute | solution.py:23
  0.5 1.1 %prepare.1 = (bf16[8,32,128]{2,1,0:T(8,128)(2,1)S(1)}, f32[8,128]{1,0:T(8,128)S(1)}, bf16[2,128,1024]{2,1,0:T(8,128)(2,1)S(1)}, f32[8,256]{1,0:T(8,128)S(1)}, bf16[2,4,16,128]{3,2,1,0:T(8,128)(2,1)S(1)}) custom-call(bf16[1,1,4096]{2,1,0:T(2,128)(2,1)} %row_hbm.1, bf16[1,1,1024]{2,1,0:T(2,128)(2,1)} %new_hbm.1, bf16[2,128,1024]{2,1,0:T(8,128)(2,1)} %pool_hbm.1, ...), custom_call_target="tpu_custom_call" | custom-call | tf_op jit(solution)/shard_map/prepare/pallas_call | solution.py:127
  1.6 10.5 %all_to_all.10.queries_ref = bf16[8,32,128]{2,1,0:T(8,128)(2,1)S(1)} all-to-all(bf16[8,32,128]{2,1,0:T(8,128)(2,1)S(1)} %get-tuple-element.10), channel_id=1, replica_groups={{5,4,3,2,1,0,7,6},{13,12,11,10,9,8,15,14},{21,20,19,18,17,16,23,22},{29..., dimensions={0} | all-to-all | bytes 131072 | tf_op jit(solution)/shard_map/all_to_all | solution.py:139
  12.2 0.0 collective-permute-done.peer_ref
  12.2 0.5 %attend.1 = f32[8,40,128]{2,1,0:T(8,128)S(1)} custom-call(bf16[8,32,128]{2,1,0:T(8,128)(2,1)S(1)} %all_to_all.10.queries_ref, bf16[2,128,1024]{2,1,0:T(8,128)(2,1)S(1)} %get-tuple-element.11.pool_ref, bf16[2,128,1024]{2,1,0:T(8,128)(2,1)S(1)} %collective-permute-done.peer_ref, f32[8,256]{1,0:T(8,128)S(1)} %get-tuple-element.12.bias_ref, ...), custom_call_target="tpu_custom_call" | custom-call | tf_op jit(solution)/shard_map/attend/pallas_call | solution.py:127
  12.7 8.8 %all_to_all.11.parts_ref = f32[8,40,128]{2,1,0:T(8,128)S(1)} all-to-all(f32[8,40,128]{2,1,0:T(8,128)S(1)} %attend.1), channel_id=1, replica_groups={{5,4,3,2,1,0,7,6},{13,12,11,10,9,8,15,14},{21,20,19,18,17,16,23,22},{29..., dimensions={0} | all-to-all | bytes 327680 | tf_op jit(solution)/shard_map/all_to_all | solution.py:139
  21.5 0.8 %settle.1 = bf16[1,1,4096]{2,1,0:T(2,128)(2,1)} custom-call(f32[8,40,128]{2,1,0:T(8,128)S(1)} %all_to_all.11.parts_ref), custom_call_target="tpu_custom_call" | custom-call | tf_op jit(solution)/shard_map/settle/pallas_call | solution.py:127
Async XLA Ops:
  0.0 12.2 %collective-permute-start = (bf16[2,128,1024]{2,1,0:T(8,128)(2,1)}, bf16[2,128,1024]{2,1,0:T(8,128)(2,1)S(1)}, u32[]{:S(2)}, u32[]{:S(2)}) collective-permute-start(bf16[2,128,1024]{2,1,0:T(8,128)(2,1)} %pool_hbm.1), channel_id=1, source_target_pairs={{0,8},{8,0},{1,9},{9,1},{2,10},{10,2},{3,11},{11,3},{4,12},{12,4},... | collective-permute-start | bytes 1572872 | tf_op jit(solution)/shard_map/ppermute | solution.py:23

commit v4 on v3

v4 whole, which is shorter than its diff:
```python
import functools

import jax
import jax.numpy as jnp
from jax import lax
from jax.experimental import pallas as pl
from jax.experimental.pallas import tpu as pltpu
from jax.sharding import PartitionSpec as P

KVH = 4
HD = 128
GROUP = 8
HQ = KVH * GROUP
STATE_ROWS = HQ + GROUP
masked_value = -1e30
GRANT = 2**24
VMEM = pltpu.VMEM
SMEM = pltpu.SMEM


def swapped(value, axis, mask):
    pairs = [(source, source ^ mask) for source in range(lax.axis_size(axis))]
    return lax.ppermute(value, axis, pairs)


def prepare_kernel(
    row_hbm, new_hbm, pool_hbm, ids_hbm, lengths_hbm, out_ref, new_ref, pool_ref, bias_ref, pick_ref, row_ref, fresh_ref, ids_ref, lengths_ref, sems
):
    slots, page_len, _ = pool_ref.shape
    moves = [(row_hbm, row_ref), (ids_hbm, ids_ref), (lengths_hbm, lengths_ref), (new_hbm, fresh_ref), (pool_hbm, pool_ref)]
    copies = [pltpu.make_async_copy(source, target, sems.at[place]) for place, (source, target) in enumerate(moves)]
    for copy in copies:
        copy.start()
    session = lax.axis_index("sess")
    column = lax.axis_index("ctx")
    copies[0].wait()
    row = row_ref[0].astype(jnp.float32).reshape(HQ, HD).astype(out_ref.dtype)
    for place in range(out_ref.shape[0]):
        out_ref[place] = row
    copies[1].wait()
    copies[2].wait()
    left = lengths_ref[session] - column * slots * page_len
    lane = lax.broadcasted_iota(jnp.int32, (bias_ref.shape[0], page_len), 1)
    idents = [ids_ref[session, 0, slot] for slot in range(slots)]
    places = [(ident // slots ^ session) * slots + ident % slots for ident in idents]
    ranks = [sum((other < place).astype(jnp.int32) for other in places) for place in places]
    for block in range(slots):
        picked, start = jnp.int32(0), jnp.int32(0)
        for slot in range(slots):
            picked = jnp.where(ranks[slot] == block, places[slot], picked)
            start = jnp.where(ranks[slot] == block, slot * page_len, start)
        bias_ref[:, block * page_len : (block + 1) * page_len] = jnp.where(lane < left - start, 0.0, masked_value)
        for later in range(slots):
            flag = jnp.where(picked == block + 1 + later, 1.0, 0.0)
            pick_ref[block, later] = jnp.full(pick_ref.shape[2:], flag, jnp.float32).astype(pick_ref.dtype)
    copies[3].wait()
    new_ref[...] = fresh_ref[0].astype(jnp.float32).reshape(2 * KVH, HD)
    copies[4].wait()


def attend_kernel(order, queries_ref, pool_ref, peer_ref, bias_ref, pick_ref, new_ref, out_ref):
    column = lax.axis_index("ctx")
    tokens = queries_ref.shape[0]
    queries = queries_ref[...].astype(jnp.float32)
    bias = bias_ref[0:1, :]
    slots, page_len, _ = pool_ref.shape
    picked = [[jnp.concatenate([pick_ref[block, later]] * (page_len // 16)) != 0 for later in range(slots)] for block in range(slots)]
    row = lax.broadcasted_iota(jnp.int32, (tokens * GROUP, 1), 0)
    token = row // GROUP
    for place, value in enumerate(order):
        token = jnp.where(row // GROUP == place, value, token)
    fresh_bias = jnp.where(token >= column, 0.0, masked_value)
    pages = [(ref, page) for ref in (pool_ref, peer_ref) for page in range(ref.shape[0])]

    def chosen(where):
        loaded = [ref[page, :, where] for ref, page in pages]
        blocks = []
        for block in range(slots):
            value = loaded[block]
            for later, mask in enumerate(picked[block]):
                value = jnp.where(mask, loaded[block + 1 + later], value)
            blocks.append(value)
        return jnp.concatenate(blocks, axis=0)

    lane = lax.broadcasted_iota(jnp.int32, (tokens * GROUP, HD), 1)
    states = jnp.zeros((tokens * GROUP, HD), jnp.float32)
    columns = [slice(place * HD, (place + 1) * HD) for place in range(2 * KVH)]
    for heads in ((0, 1, 2, 3),):
        found = []
        for head in heads:
            query = queries[:, head * GROUP : (head + 1) * GROUP, :].reshape(tokens * GROUP, HD)
            scores = lax.dot_general(
                query.astype(jnp.bfloat16), chosen(columns[head]), (((1,), (1,)), ((), ())), preferred_element_type=jnp.float32
            )
            scores = scores * HD ** (-0.5) + bias
            fresh_scores = jnp.sum(query * new_ref[head : head + 1, :], axis=1, keepdims=True) * HD ** (-0.5) + fresh_bias
            found.append((scores, fresh_scores))
        tops = [jnp.maximum(jnp.max(scores, axis=1, keepdims=True), fresh_scores) for scores, fresh_scores in found]
        for head, (scores, fresh_scores), top in zip(heads, found, tops):
            weights = jnp.exp(scores - top)
            fresh_weights = jnp.exp(fresh_scores - top)
            total = jnp.sum(weights, axis=1, keepdims=True) + fresh_weights
            coarse = weights.astype(jnp.bfloat16)
            fine = (weights - coarse.astype(jnp.float32)).astype(jnp.bfloat16)
            values = chosen(columns[KVH + head])
            summed = (
                jnp.dot(coarse, values, preferred_element_type=jnp.float32)
                + jnp.dot(fine, values, preferred_element_type=jnp.float32)
                + fresh_weights * new_ref[KVH + head : KVH + head + 1, :]
            )
            states = jnp.where(lane == head, top, states)
            states = jnp.where(lane == KVH + head, total, states)
            out_ref[:, head * GROUP : (head + 1) * GROUP, :] = summed.reshape(tokens, GROUP, HD)
    out_ref[:, HQ:, :] = states.reshape(tokens, GROUP, HD)


def settle_kernel(parts_ref, out_ref):
    devices = parts_ref.shape[0]
    tops = [parts_ref[source, HQ:, :] for source in range(devices)]
    highest = functools.reduce(jnp.maximum, tops)
    weight_sum = 0.0
    factors = []
    for states in tops:
        factor = jnp.exp(states - highest)
        factors.append(factor)
        weight_sum = weight_sum + pltpu.roll(states, HD - KVH, 1) * factor
    pieces = []
    for head in range(KVH):
        summed = 0.0
        for source in range(devices):
            summed = summed + parts_ref[source, head * GROUP : (head + 1) * GROUP, :] * factors[source][:, head : head + 1]
        pieces.append(summed / weight_sum[:, head : head + 1])
    result = jnp.concatenate(pieces, axis=0)
    out_ref[0] = result.reshape(1, HQ * HD).astype(out_ref.dtype)


def kernel_call(kernel, out_shape, *operands, name, space=VMEM, scratch=()):
    return pl.pallas_call(
        kernel,
        out_shape=out_shape,
        in_specs=[pl.BlockSpec(memory_space=space) for _ in operands],
        out_specs=jax.tree.map(lambda _: pl.BlockSpec(memory_space=VMEM), out_shape),
        scratch_shapes=scratch,
        name=name,
        compiler_params=pltpu.CompilerParams(vmem_limit_bytes=GRANT),
    )(*operands)


def exchanged(value, order):
    return lax.all_to_all(value, "ctx", split_axis=0, concat_axis=0, axis_index_groups=[order], tiled=True)


def body(queries, new_kv, kv_pool, page_ids, cached_lengths):
    devices = lax.axis_size("ctx")
    order = [(devices // 2 + 1 - place) % devices for place in range(devices)]
    shape = jax.ShapeDtypeStruct
    peer_pool = swapped(kv_pool, "sess", 1)
    slots, page_len, width = kv_pool.shape
    spread, fresh, pool, bias, pick = kernel_call(
        prepare_kernel,
        (
            shape((devices, HQ, HD), queries.dtype),
            shape((2 * KVH, HD), jnp.float32),
            shape(kv_pool.shape, kv_pool.dtype),
            shape((8, slots * page_len), jnp.float32),
            shape((slots, slots, 16, HD), kv_pool.dtype),
        ),
        *(pltpu.with_memory_space_constraint(value, pltpu.HBM) for value in (queries, new_kv, kv_pool, page_ids, cached_lengths)), name="prepare", space=pltpu.HBM,
        scratch=[
            VMEM(queries.shape, queries.dtype), VMEM(new_kv.shape, new_kv.dtype), SMEM(page_ids.shape, jnp.int32),
            SMEM(cached_lengths.shape, jnp.int32), pltpu.SemaphoreType.DMA((5,)),
        ],
    )
    gathered = exchanged(spread, order)
    states = kernel_call(
        functools.partial(attend_kernel, order), shape((devices, STATE_ROWS, HD), jnp.float32),
        gathered, pool, peer_pool, bias, pick, fresh, name="attend",
    )
    parts = exchanged(states, order)
    return kernel_call(settle_kernel, shape(queries.shape, queries.dtype), parts, name="settle")


def solution(mesh):
    placed = (
        P(("groups", "sess"), "ctx", None),
        P(("groups", "sess"), "ctx", None),
        P(("groups", "sess", "ctx"), None, None),
        P("groups", "ctx", None),
        P("groups"),
    )
    return jax.shard_map(body, mesh=mesh, in_specs=placed, out_specs=P(("groups", "sess"), "ctx", None), check_vma=False)
```

time: 22.6 us -> 22.6 us (level)
  no operation moved by 1% of the time
where the time goes in v4:
time: 22.6 us; the launch traced here: 22.3 us
  blocking collectives  19.4 us (86%)
  Pallas kernels  2.39 us (11%)
  starting transfers between devices  0.49 us (2%)
    all_to_all x2, blocking collectives, exchanged(): lax.all_to_all(value, 'ctx', split_axis=0, concat_axis=0, axis_index_grou...  19.4 us
    pallas_call x3, Pallas kernels, kernel_call(): pl.pallas_call(kernel, out_shape=out_shape, in_specs=[pl.BlockSpec(memory...  2.39 us
    ppermute x1, starting transfers between devices, swapped(): return lax.ppermute(value, axis, pairs)  0.49 us
  transfers between devices with their start and end apart: 1, of which 0 were waited for; matrix products, arithmetic and copies ran while one was open for 0% of the time, Pallas kernels for 5%

profile of v4, /device:TPU:0, one launch (start us, length us, event | category | flops | bytes accessed | tf_op | source)
XLA Modules:
  0.0 22.3 jit_solution(766918954349798274)
XLA Ops:
  0.0 0.5 %collective-permute-start = (bf16[2,128,1024]{2,1,0:T(8,128)(2,1)}, bf16[2,128,1024]{2,1,0:T(8,128)(2,1)S(1)}, u32[]{:S(2)}, u32[]{:S(2)}) collective-permute-start(bf16[2,128,1024]{2,1,0:T(8,128)(2,1)} %pool_hbm.1), channel_id=1, source_target_pairs={{0,8},{8,0},{1,9},{9,1},{2,10},{10,2},{3,11},{11,3},{4,12},{12,4},... | collective-permute-start | bytes 1572872 | tf_op jit(solution)/shard_map/ppermute | solution.py:23
  0.5 1.1 %prepare.1 = (bf16[8,32,128]{2,1,0:T(8,128)(2,1)S(1)}, f32[8,128]{1,0:T(8,128)S(1)}, bf16[2,128,1024]{2,1,0:T(8,128)(2,1)S(1)}, f32[8,256]{1,0:T(8,128)S(1)}, bf16[2,2,16,128]{3,2,1,0:T(8,128)(2,1)S(1)}) custom-call(bf16[1,1,4096]{2,1,0:T(2,128)(2,1)} %row_hbm.1, bf16[1,1,1024]{2,1,0:T(2,128)(2,1)} %new_hbm.1, bf16[2,128,1024]{2,1,0:T(8,128)(2,1)} %pool_hbm.1, ...), custom_call_target="tpu_custom_call" | custom-call | tf_op jit(solution)/shard_map/prepare/pallas_call | solution.py:138
  1.6 10.5 %all_to_all.10.queries_ref = bf16[8,32,128]{2,1,0:T(8,128)(2,1)S(1)} all-to-all(bf16[8,32,128]{2,1,0:T(8,128)(2,1)S(1)} %get-tuple-element.10), channel_id=1, replica_groups={{5,4,3,2,1,0,7,6},{13,12,11,10,9,8,15,14},{21,20,19,18,17,16,23,22},{29..., dimensions={0} | all-to-all | bytes 131072 | tf_op jit(solution)/shard_map/all_to_all | solution.py:150
  12.2 0.0 collective-permute-done.peer_ref
  12.2 0.5 %attend.1 = f32[8,40,128]{2,1,0:T(8,128)S(1)} custom-call(bf16[8,32,128]{2,1,0:T(8,128)(2,1)S(1)} %all_to_all.10.queries_ref, bf16[2,128,1024]{2,1,0:T(8,128)(2,1)S(1)} %get-tuple-element.11.pool_ref, bf16[2,128,1024]{2,1,0:T(8,128)(2,1)S(1)} %collective-permute-done.peer_ref, f32[8,256]{1,0:T(8,128)S(1)} %get-tuple-element.12.bias_ref, ...), custom_call_target="tpu_custom_call" | custom-call | tf_op jit(solution)/shard_map/attend/pallas_call | solution.py:138
  12.7 8.8 %all_to_all.11.parts_ref = f32[8,40,128]{2,1,0:T(8,128)S(1)} all-to-all(f32[8,40,128]{2,1,0:T(8,128)S(1)} %attend.1), channel_id=1, replica_groups={{5,4,3,2,1,0,7,6},{13,12,11,10,9,8,15,14},{21,20,19,18,17,16,23,22},{29..., dimensions={0} | all-to-all | bytes 327680 | tf_op jit(solution)/shard_map/all_to_all | solution.py:150
  21.5 0.8 %settle.1 = bf16[1,1,4096]{2,1,0:T(2,128)(2,1)} custom-call(f32[8,40,128]{2,1,0:T(8,128)S(1)} %all_to_all.11.parts_ref), custom_call_target="tpu_custom_call" | custom-call | tf_op jit(solution)/shard_map/settle/pallas_call | solution.py:138
Async XLA Ops:
  0.0 12.2 %collective-permute-start = (bf16[2,128,1024]{2,1,0:T(8,128)(2,1)}, bf16[2,128,1024]{2,1,0:T(8,128)(2,1)S(1)}, u32[]{:S(2)}, u32[]{:S(2)}) collective-permute-start(bf16[2,128,1024]{2,1,0:T(8,128)(2,1)} %pool_hbm.1), channel_id=1, source_target_pairs={{0,8},{8,0},{1,9},{9,1},{2,10},{10,2},{3,11},{11,3},{4,12},{12,4},... | collective-permute-start | bytes 1572872 | tf_op jit(solution)/shard_map/ppermute | solution.py:23

commit v5 on v4

--- a/solution.py
+++ b/solution.py
@@ -29,7 +29,7 @@
     slots, page_len, _ = pool_ref.shape
     moves = [(row_hbm, row_ref), (ids_hbm, ids_ref), (lengths_hbm, lengths_ref), (new_hbm, fresh_ref), (pool_hbm, pool_ref)]
     copies = [pltpu.make_async_copy(source, target, sems.at[place]) for place, (source, target) in enumerate(moves)]
-    for copy in copies:
+    for copy in copies[::-1]:
         copy.start()
     session = lax.axis_index("sess")
     column = lax.axis_index("ctx")

time: 22.6 us -> 22.5 us (level)
  no operation moved by 1% of the time
where the time goes in v5:
time: 22.5 us; the launch traced here: 22.2 us
  blocking collectives  19.4 us (86%)
  Pallas kernels  2.35 us (10%)
  starting transfers between devices  0.49 us (2%)
    all_to_all x2, blocking collectives, exchanged(): lax.all_to_all(value, 'ctx', split_axis=0, concat_axis=0, axis_index_grou...  19.4 us
    pallas_call x3, Pallas kernels, kernel_call(): pl.pallas_call(kernel, out_shape=out_shape, in_specs=[pl.BlockSpec(memory...  2.35 us
    ppermute x1, starting transfers between devices, swapped(): return lax.ppermute(value, axis, pairs)  0.49 us
  transfers between devices with their start and end apart: 1, of which 0 were waited for; matrix products, arithmetic and copies ran while one was open for 0% of the time, Pallas kernels for 5%

profile of v5, /device:TPU:0, one launch (start us, length us, event | category | flops | bytes accessed | tf_op | source)
XLA Modules:
  0.0 22.2 jit_solution(255657664019422369)
XLA Ops:
  0.0 0.5 %collective-permute-start = (bf16[2,128,1024]{2,1,0:T(8,128)(2,1)}, bf16[2,128,1024]{2,1,0:T(8,128)(2,1)S(1)}, u32[]{:S(2)}, u32[]{:S(2)}) collective-permute-start(bf16[2,128,1024]{2,1,0:T(8,128)(2,1)} %pool_hbm.1), channel_id=1, source_target_pairs={{0,8},{8,0},{1,9},{9,1},{2,10},{10,2},{3,11},{11,3},{4,12},{12,4},... | collective-permute-start | bytes 1572872 | tf_op jit(solution)/shard_map/ppermute | solution.py:23
  0.5 1.1 %prepare.1 = (bf16[8,32,128]{2,1,0:T(8,128)(2,1)S(1)}, f32[8,128]{1,0:T(8,128)S(1)}, bf16[2,128,1024]{2,1,0:T(8,128)(2,1)S(1)}, f32[8,256]{1,0:T(8,128)S(1)}, bf16[2,2,16,128]{3,2,1,0:T(8,128)(2,1)S(1)}) custom-call(bf16[1,1,4096]{2,1,0:T(2,128)(2,1)} %row_hbm.1, bf16[1,1,1024]{2,1,0:T(2,128)(2,1)} %new_hbm.1, bf16[2,128,1024]{2,1,0:T(8,128)(2,1)} %pool_hbm.1, ...), custom_call_target="tpu_custom_call" | custom-call | tf_op jit(solution)/shard_map/prepare/pallas_call | solution.py:138
  1.6 10.5 %all_to_all.10.queries_ref = bf16[8,32,128]{2,1,0:T(8,128)(2,1)S(1)} all-to-all(bf16[8,32,128]{2,1,0:T(8,128)(2,1)S(1)} %get-tuple-element.10), channel_id=1, replica_groups={{5,4,3,2,1,0,7,6},{13,12,11,10,9,8,15,14},{21,20,19,18,17,16,23,22},{29..., dimensions={0} | all-to-all | bytes 131072 | tf_op jit(solution)/shard_map/all_to_all | solution.py:150
  12.1 0.0 collective-permute-done.peer_ref
  12.1 0.5 %attend.1 = f32[8,40,128]{2,1,0:T(8,128)S(1)} custom-call(bf16[8,32,128]{2,1,0:T(8,128)(2,1)S(1)} %all_to_all.10.queries_ref, bf16[2,128,1024]{2,1,0:T(8,128)(2,1)S(1)} %get-tuple-element.11.pool_ref, bf16[2,128,1024]{2,1,0:T(8,128)(2,1)S(1)} %collective-permute-done.peer_ref, f32[8,256]{1,0:T(8,128)S(1)} %get-tuple-element.12.bias_ref, ...), custom_call_target="tpu_custom_call" | custom-call | tf_op jit(solution)/shard_map/attend/pallas_call | solution.py:138
  12.6 8.8 %all_to_all.11.parts_ref = f32[8,40,128]{2,1,0:T(8,128)S(1)} all-to-all(f32[8,40,128]{2,1,0:T(8,128)S(1)} %attend.1), channel_id=1, replica_groups={{5,4,3,2,1,0,7,6},{13,12,11,10,9,8,15,14},{21,20,19,18,17,16,23,22},{29..., dimensions={0} | all-to-all | bytes 327680 | tf_op jit(solution)/shard_map/all_to_all | solution.py:150
  21.5 0.8 %settle.1 = bf16[1,1,4096]{2,1,0:T(2,128)(2,1)} custom-call(f32[8,40,128]{2,1,0:T(8,128)S(1)} %all_to_all.11.parts_ref), custom_call_target="tpu_custom_call" | custom-call | tf_op jit(solution)/shard_map/settle/pallas_call | solution.py:138
Async XLA Ops:
  0.0 12.1 %collective-permute-start = (bf16[2,128,1024]{2,1,0:T(8,128)(2,1)}, bf16[2,128,1024]{2,1,0:T(8,128)(2,1)S(1)}, u32[]{:S(2)}, u32[]{:S(2)}) collective-permute-start(bf16[2,128,1024]{2,1,0:T(8,128)(2,1)} %pool_hbm.1), channel_id=1, source_target_pairs={{0,8},{8,0},{1,9},{9,1},{2,10},{10,2},{3,11},{11,3},{4,12},{12,4},... | collective-permute-start | bytes 1572872 | tf_op jit(solution)/shard_map/ppermute | solution.py:23

commit v6 on v5

--- a/solution.py
+++ b/solution.py
@@ -12,7 +12,7 @@
 GROUP = 8
 HQ = KVH * GROUP
 STATE_ROWS = HQ + GROUP
-masked_value = -1e30
+masked_value = -30000.0
 GRANT = 2**24
 VMEM = pltpu.VMEM
 SMEM = pltpu.SMEM
@@ -58,6 +58,16 @@
     copies[4].wait()
 
 
+def pieces_of(value):
+    parts = []
+    for _ in range(2):
+        scaled = value * 8193.0
+        part = scaled - (scaled - value)
+        parts.append(part)
+        value = value - part
+    return parts + [value]
+
+
 def attend_kernel(order, queries_ref, pool_ref, peer_ref, bias_ref, pick_ref, new_ref, out_ref):
     column = lax.axis_index("ctx")
     tokens = queries_ref.shape[0]
@@ -101,29 +111,30 @@
             fresh_weights = jnp.exp(fresh_scores - top)
             total = jnp.sum(weights, axis=1, keepdims=True) + fresh_weights
             coarse = weights.astype(jnp.bfloat16)
-            fine = (weights - coarse.astype(jnp.float32)).astype(jnp.bfloat16)
             values = chosen(columns[KVH + head])
             summed = (
                 jnp.dot(coarse, values, preferred_element_type=jnp.float32)
-                + jnp.dot(fine, values, preferred_element_type=jnp.float32)
                 + fresh_weights * new_ref[KVH + head : KVH + head + 1, :]
             )
-            states = jnp.where(lane == head, top, states)
-            states = jnp.where(lane == KVH + head, total, states)
+            peak = jnp.maximum(jnp.max(jnp.abs(summed), axis=1, keepdims=True), 1e-30)
+            summed = summed / peak
+            for place, part in enumerate(pieces_of(top + jnp.log(total)) + pieces_of(jnp.log(peak / total))):
+                states = jnp.where(lane == place * KVH + head, part, states)
             out_ref[:, head * GROUP : (head + 1) * GROUP, :] = summed.reshape(tokens, GROUP, HD)
     out_ref[:, HQ:, :] = states.reshape(tokens, GROUP, HD)
 
 
 def settle_kernel(parts_ref, out_ref):
     devices = parts_ref.shape[0]
-    tops = [parts_ref[source, HQ:, :] for source in range(devices)]
+    found = [parts_ref[source, HQ:, :] for source in range(devices)]
+    tops = [sum((pltpu.roll(states, HD - place * KVH, 1) for place in (1, 2)), states) for states in found]
+    peaks = [sum(pltpu.roll(states, HD - place * KVH, 1) for place in (3, 4, 5)) for states in found]
     highest = functools.reduce(jnp.maximum, tops)
     weight_sum = 0.0
     factors = []
-    for states in tops:
-        factor = jnp.exp(states - highest)
-        factors.append(factor)
-        weight_sum = weight_sum + pltpu.roll(states, HD - KVH, 1) * factor
+    for top, peak in zip(tops, peaks):
+        factors.append(jnp.exp(top - highest + peak))
+        weight_sum = weight_sum + jnp.exp(top - highest)
     pieces = []
     for head in range(KVH):
         summed = 0.0
@@ -176,7 +187,7 @@
         functools.partial(attend_kernel, order), shape((devices, STATE_ROWS, HD), jnp.float32),
         gathered, pool, peer_pool, bias, pick, fresh, name="attend",
     )
-    parts = exchanged(states, order)
+    parts = exchanged(states.astype(jnp.float16), order).astype(jnp.float32)
     return kernel_call(settle_kernel, shape(queries.shape, queries.dtype), parts, name="settle")
 
 

time: 22.5 us -> 22.4 us (level)
  blocking collectives: 19.4 us -> 19.1 us
    all_to_all x2, blocking collectives: 19.4 us -> 19.1 us  [exchanged(): lax.all_to_all(value, 'ctx', split_axis=0, concat_axis=0, axis_index_grou...]
where the time goes in v6:
time: 22.4 us; the launch traced here: 22.2 us
  blocking collectives  19.1 us (85%)
  Pallas kernels  2.51 us (11%)
  starting transfers between devices  0.49 us (2%)
    all_to_all x2, blocking collectives, exchanged(): lax.all_to_all(value, 'ctx', split_axis=0, concat_axis=0, axis_index_grou...  19.1 us
    pallas_call x3, Pallas kernels, kernel_call(): pl.pallas_call(kernel, out_shape=out_shape, in_specs=[pl.BlockSpec(memory...  2.51 us
    ppermute x1, starting transfers between devices, swapped(): return lax.ppermute(value, axis, pairs)  0.49 us
  transfers between devices with their start and end apart: 1, of which 0 were waited for; matrix products, arithmetic and copies ran while one was open for 0% of the time, Pallas kernels for 5%

profile of v6, /device:TPU:0, one launch (start us, length us, event | category | flops | bytes accessed | tf_op | source)
XLA Modules:
  0.0 22.2 jit_solution(4583765289072200233)
XLA Ops:
  0.0 0.5 %collective-permute-start = (bf16[2,128,1024]{2,1,0:T(8,128)(2,1)}, bf16[2,128,1024]{2,1,0:T(8,128)(2,1)S(1)}, u32[]{:S(2)}, u32[]{:S(2)}) collective-permute-start(bf16[2,128,1024]{2,1,0:T(8,128)(2,1)} %pool_hbm.1), channel_id=1, source_target_pairs={{0,8},{8,0},{1,9},{9,1},{2,10},{10,2},{3,11},{11,3},{4,12},{12,4},... | collective-permute-start | bytes 1572872 | tf_op jit(solution)/shard_map/ppermute | solution.py:23
  0.5 1.1 %prepare.1 = (bf16[8,32,128]{2,1,0:T(8,128)(2,1)S(1)}, f32[8,128]{1,0:T(8,128)S(1)}, bf16[2,128,1024]{2,1,0:T(8,128)(2,1)S(1)}, f32[8,256]{1,0:T(8,128)S(1)}, bf16[2,2,16,128]{3,2,1,0:T(8,128)(2,1)S(1)}) custom-call(bf16[1,1,4096]{2,1,0:T(2,128)(2,1)} %row_hbm.1, bf16[1,1,1024]{2,1,0:T(2,128)(2,1)} %new_hbm.1, bf16[2,128,1024]{2,1,0:T(8,128)(2,1)} %pool_hbm.1, ...), custom_call_target="tpu_custom_call" | custom-call | tf_op jit(solution)/shard_map/prepare/pallas_call | solution.py:149
  1.6 10.5 %all_to_all.10.queries_ref = bf16[8,32,128]{2,1,0:T(8,128)(2,1)S(1)} all-to-all(bf16[8,32,128]{2,1,0:T(8,128)(2,1)S(1)} %get-tuple-element.10), channel_id=1, replica_groups={{5,4,3,2,1,0,7,6},{13,12,11,10,9,8,15,14},{21,20,19,18,17,16,23,22},{29..., dimensions={0} | all-to-all | bytes 131072 | tf_op jit(solution)/shard_map/all_to_all | solution.py:161
  12.1 0.0 collective-permute-done.peer_ref
  12.1 0.6 %attend.1 = f32[8,40,128]{2,1,0:T(8,128)S(1)} custom-call(bf16[8,32,128]{2,1,0:T(8,128)(2,1)S(1)} %all_to_all.10.queries_ref, bf16[2,128,1024]{2,1,0:T(8,128)(2,1)S(1)} %get-tuple-element.11.pool_ref, bf16[2,128,1024]{2,1,0:T(8,128)(2,1)S(1)} %collective-permute-done.peer_ref, f32[8,256]{1,0:T(8,128)S(1)} %get-tuple-element.12.bias_ref, ...), custom_call_target="tpu_custom_call" | custom-call | tf_op jit(solution)/shard_map/attend/pallas_call | solution.py:149
  12.7 8.6 %all_to_all.11 = f16[8,40,128]{2,1,0:T(8,128)(2,1)S(1)} all-to-all(f16[8,40,128]{2,1,0:T(8,128)(2,1)S(1)} %convert_element_type.6), channel_id=1, replica_groups={{5,4,3,2,1,0,7,6},{13,12,11,10,9,8,15,14},{21,20,19,18,17,16,23,22},{29..., dimensions={0} | all-to-all | bytes 163840 | tf_op jit(solution)/shard_map/all_to_all | solution.py:161
  21.3 0.8 %settle.1 = bf16[1,1,4096]{2,1,0:T(2,128)(2,1)} custom-call(f32[8,40,128]{2,1,0:T(8,128)S(1)} %convert_element_type.7.parts_ref), custom_call_target="tpu_custom_call" | custom-call | tf_op jit(solution)/shard_map/settle/pallas_call | solution.py:149
  (2 shorter events, 0.0 us)
Async XLA Ops:
  0.0 12.1 %collective-permute-start = (bf16[2,128,1024]{2,1,0:T(8,128)(2,1)}, bf16[2,128,1024]{2,1,0:T(8,128)(2,1)S(1)}, u32[]{:S(2)}, u32[]{:S(2)}) collective-permute-start(bf16[2,128,1024]{2,1,0:T(8,128)(2,1)} %pool_hbm.1), channel_id=1, source_target_pairs={{0,8},{8,0},{1,9},{9,1},{2,10},{10,2},{3,11},{11,3},{4,12},{12,4},... | collective-permute-start | bytes 1572872 | tf_op jit(solution)/shard_map/ppermute | solution.py:23

commit v7 on v5

--- a/solution.py
+++ b/solution.py
@@ -97,15 +97,13 @@
             found.append((scores, fresh_scores))
         tops = [jnp.maximum(jnp.max(scores, axis=1, keepdims=True), fresh_scores) for scores, fresh_scores in found]
         for head, (scores, fresh_scores), top in zip(heads, found, tops):
-            weights = jnp.exp(scores - top)
+            coarse = jnp.exp(scores - top).astype(jnp.bfloat16)
             fresh_weights = jnp.exp(fresh_scores - top)
-            total = jnp.sum(weights, axis=1, keepdims=True) + fresh_weights
-            coarse = weights.astype(jnp.bfloat16)
-            fine = (weights - coarse.astype(jnp.float32)).astype(jnp.bfloat16)
             values = chosen(columns[KVH + head])
+            both = jnp.dot(coarse, jnp.concatenate([values, jnp.ones_like(values)], axis=1), preferred_element_type=jnp.float32)
+            total = both[:, HD:] + fresh_weights
             summed = (
-                jnp.dot(coarse, values, preferred_element_type=jnp.float32)
-                + jnp.dot(fine, values, preferred_element_type=jnp.float32)
+                both[:, :HD]
                 + fresh_weights * new_ref[KVH + head : KVH + head + 1, :]
             )
             states = jnp.where(lane == head, top, states)

time: 22.5 us -> 22.5 us (level)
  no operation moved by 1% of the time
where the time goes in v7:
time: 22.5 us; the launch traced here: 22.2 us
  blocking collectives  19.4 us (86%)
  Pallas kernels  2.31 us (10%)
  starting transfers between devices  0.49 us (2%)
    all_to_all x2, blocking collectives, exchanged(): lax.all_to_all(value, 'ctx', split_axis=0, concat_axis=0, axis_index_grou...  19.4 us
    pallas_call x3, Pallas kernels, kernel_call(): pl.pallas_call(kernel, out_shape=out_shape, in_specs=[pl.BlockSpec(memory...  2.31 us
    ppermute x1, starting transfers between devices, swapped(): return lax.ppermute(value, axis, pairs)  0.49 us
  transfers between devices with their start and end apart: 1, of which 0 were waited for; matrix products, arithmetic and copies ran while one was open for 0% of the time, Pallas kernels for 5%

profile of v7, /device:TPU:0, one launch (start us, length us, event | category | flops | bytes accessed | tf_op | source)
XLA Modules:
  0.0 22.2 jit_solution(11487660297243979663)
XLA Ops:
  0.0 0.5 %collective-permute-start = (bf16[2,128,1024]{2,1,0:T(8,128)(2,1)}, bf16[2,128,1024]{2,1,0:T(8,128)(2,1)S(1)}, u32[]{:S(2)}, u32[]{:S(2)}) collective-permute-start(bf16[2,128,1024]{2,1,0:T(8,128)(2,1)} %pool_hbm.1), channel_id=1, source_target_pairs={{0,8},{8,0},{1,9},{9,1},{2,10},{10,2},{3,11},{11,3},{4,12},{12,4},... | collective-permute-start | bytes 1572872 | tf_op jit(solution)/shard_map/ppermute | solution.py:23
  0.5 1.1 %prepare.1 = (bf16[8,32,128]{2,1,0:T(8,128)(2,1)S(1)}, f32[8,128]{1,0:T(8,128)S(1)}, bf16[2,128,1024]{2,1,0:T(8,128)(2,1)S(1)}, f32[8,256]{1,0:T(8,128)S(1)}, bf16[2,2,16,128]{3,2,1,0:T(8,128)(2,1)S(1)}) custom-call(bf16[1,1,4096]{2,1,0:T(2,128)(2,1)} %row_hbm.1, bf16[1,1,1024]{2,1,0:T(2,128)(2,1)} %new_hbm.1, bf16[2,128,1024]{2,1,0:T(8,128)(2,1)} %pool_hbm.1, ...), custom_call_target="tpu_custom_call" | custom-call | tf_op jit(solution)/shard_map/prepare/pallas_call | solution.py:136
  1.6 10.5 %all_to_all.10.queries_ref = bf16[8,32,128]{2,1,0:T(8,128)(2,1)S(1)} all-to-all(bf16[8,32,128]{2,1,0:T(8,128)(2,1)S(1)} %get-tuple-element.10), channel_id=1, replica_groups={{5,4,3,2,1,0,7,6},{13,12,11,10,9,8,15,14},{21,20,19,18,17,16,23,22},{29..., dimensions={0} | all-to-all | bytes 131072 | tf_op jit(solution)/shard_map/all_to_all | solution.py:148
  12.1 0.0 collective-permute-done.peer_ref
  12.1 0.4 %attend.1 = f32[8,40,128]{2,1,0:T(8,128)S(1)} custom-call(bf16[8,32,128]{2,1,0:T(8,128)(2,1)S(1)} %all_to_all.10.queries_ref, bf16[2,128,1024]{2,1,0:T(8,128)(2,1)S(1)} %get-tuple-element.11.pool_ref, bf16[2,128,1024]{2,1,0:T(8,128)(2,1)S(1)} %collective-permute-done.peer_ref, f32[8,256]{1,0:T(8,128)S(1)} %get-tuple-element.12.bias_ref, ...), custom_call_target="tpu_custom_call" | custom-call | tf_op jit(solution)/shard_map/attend/pallas_call | solution.py:136
  12.6 8.8 %all_to_all.11.parts_ref = f32[8,40,128]{2,1,0:T(8,128)S(1)} all-to-all(f32[8,40,128]{2,1,0:T(8,128)S(1)} %attend.1), channel_id=1, replica_groups={{5,4,3,2,1,0,7,6},{13,12,11,10,9,8,15,14},{21,20,19,18,17,16,23,22},{29..., dimensions={0} | all-to-all | bytes 327680 | tf_op jit(solution)/shard_map/all_to_all | solution.py:148
  21.4 0.8 %settle.1 = bf16[1,1,4096]{2,1,0:T(2,128)(2,1)} custom-call(f32[8,40,128]{2,1,0:T(8,128)S(1)} %all_to_all.11.parts_ref), custom_call_target="tpu_custom_call" | custom-call | tf_op jit(solution)/shard_map/settle/pallas_call | solution.py:136
Async XLA Ops:
  0.0 12.1 %collective-permute-start = (bf16[2,128,1024]{2,1,0:T(8,128)(2,1)}, bf16[2,128,1024]{2,1,0:T(8,128)(2,1)S(1)}, u32[]{:S(2)}, u32[]{:S(2)}) collective-permute-start(bf16[2,128,1024]{2,1,0:T(8,128)(2,1)} %pool_hbm.1), channel_id=1, source_target_pairs={{0,8},{8,0},{1,9},{9,1},{2,10},{10,2},{3,11},{11,3},{4,12},{12,4},... | collective-permute-start | bytes 1572872 | tf_op jit(solution)/shard_map/ppermute | solution.py:23
